TPU v7x, 256 devices: a whole 4x4x8 slice. The times are simulated.
256 devices in a mesh: dp: 8 (over y, core), fsdp: 32 (over x, z).
Axes of the slice: x: 4, y: 4, z: 8, core: 2. Of those that a mesh axis runs over, the one named last changes fastest.
Arguments:
- acts: bfloat16 [32768, 8192], P(('dp', 'fsdp')), may hold values from -3 to 3
- out_grads: bfloat16 [32768, 8192], P(('dp', 'fsdp')), may hold values from -6 to 6
- token_counts: int32 [8], replicated, may hold values from 2048 to 4096, as said below
- k_factor: float32 [32, 256, 512], P('fsdp'), may hold values from -0.1875 to 2.44
- c_factor: float32 [32, 256, 512], P('fsdp'), may hold values from -0.1875 to 2.44
- k_moment: float32 [32, 256, 512], P('fsdp'), may hold values from -0.046875 to 0.946875
- c_moment: float32 [32, 256, 512], P('fsdp'), may hold values from -0.046875 to 0.946875
- grad_weight: bfloat16 [8192, 8192], P('dp', 'fsdp'), may hold values from -6 to 6
Outputs:
- k_factor_new: float32 [32, 256, 512], P('fsdp')
- c_factor_new: float32 [32, 256, 512], P('fsdp')
- k_moment_new: float32 [32, 256, 512], P('fsdp')
- c_moment_new: float32 [32, 256, 512], P('fsdp')
- precond: bfloat16 [8192, 8192], P('dp', 'fsdp')
Inputs may be any that keep to these rules, and one draw needn't show every extreme that they name: `token_counts`: some data group has all 4096 slots valid and some other has exactly 2048.
All inputs are finite; a program needn't handle non-finite values.
Results may differ from a plain program's by a relative error of at most 0.0081.
Values may be sent and summed in bfloat16 or wider, within the bound.
A program may use at most 64 MiB of HBM per device.

v0:
```python
import jax
import jax.numpy as jnp
from jax import lax
from jax.sharding import PartitionSpec as P

damping = 0.1
momentum_rate = 0.5
step_rate = 0.2
highest = lax.Precision.HIGHEST


def spread(value, axis, source):
    kept = jnp.where(lax.axis_index(axis) == source, value, 0).astype(value.dtype)
    return lax.psum(kept, axis)


def owner_image(columns, lead_columns, diag_half, side_half):
    row_count = columns.shape[0]
    block_count = diag_half.shape[0]
    block_size = diag_half.shape[1]
    blocked = columns.reshape(row_count, block_count, block_size)
    image_sum = jnp.einsum("tnk,nkj->tnj", blocked, diag_half, preferred_element_type=jnp.float32)
    image_sum = image_sum + jnp.einsum(
        "tk,nkj->tnj", lead_columns, side_half, preferred_element_type=jnp.float32
    )
    return image_sum.astype(jnp.bfloat16).reshape(row_count, block_count * block_size)


def to_owners(pair):
    return (
        lax.all_to_all(pair[0], "fsdp", split_axis=1, concat_axis=0, tiled=True),
        lax.all_to_all(pair[1], "fsdp", split_axis=1, concat_axis=0, tiled=True),
    )


def fetch_lead(after):
    return (spread(after[0], "fsdp", 0), spread(after[1], "fsdp", 0))


def block_stats(owned, lead_image, block_count, block_size):
    blocked = owned.reshape(owned.shape[0], block_count, block_size)
    own_sum = jnp.einsum("tni,tnj->nij", blocked, blocked, preferred_element_type=jnp.float32)
    cross_sum = jnp.einsum("ti,tnj->nij", lead_image, blocked, preferred_element_type=jnp.float32)
    return (own_sum, cross_sum)


def gram_trace(factor, border_keep):
    block_size = factor.shape[1]
    diag_part = factor[:, :, :block_size]
    side_part = factor[:, :, block_size:] * border_keep
    return jnp.sum(diag_part * diag_part) + jnp.sum(side_part * side_part)


def advance(factor, moment, own_sum, cross_sum, lead_block, border_keep, other_h, other_g, width):
    block_size = factor.shape[1]
    diag_part = factor[:, :, :block_size]
    side_part = factor[:, :, block_size:] * border_keep
    gram_diag = jnp.einsum("nki,nkj->nij", diag_part, diag_part, precision=highest)
    gram_diag = gram_diag + jnp.einsum("nki,nkj->nij", side_part, side_part, precision=highest)
    gram_side = jnp.einsum("ki,nkj->nij", lead_block, side_part, precision=highest)
    identity = jnp.eye(block_size, dtype=jnp.float32)
    fresh_diag = (other_h * own_sum + damping * other_g * gram_diag - width * identity) / (
        2.0 * width
    )
    fresh_side = (other_h * cross_sum + damping * other_g * gram_side) * border_keep / (2.0 * width)
    moment_diag = momentum_rate * moment[:, :, :block_size] + fresh_diag
    moment_side = (momentum_rate * moment[:, :, block_size:] + fresh_side) * border_keep
    new_diag = diag_part - step_rate * jnp.einsum(
        "nik,nkj->nij", diag_part, moment_diag, precision=highest
    )
    side_change = jnp.einsum("ik,nkj->nij", lead_block, moment_side, precision=highest)
    side_change = side_change + jnp.einsum(
        "nik,nkj->nij", side_part, moment_diag, precision=highest
    )
    new_side = (side_part - step_rate * side_change) * border_keep
    return (
        jnp.concatenate([new_diag, new_side], axis=-1),
        jnp.concatenate([moment_diag, moment_side], axis=-1),
    )


def per_device(acts, out_grads, token_counts, k_factor, c_factor, k_moment, c_moment, grad_weight):
    tok_dev, width = acts.shape
    blocks_dev = k_factor.shape[0]
    block_size = k_factor.shape[1]
    group_count = lax.axis_size("dp")
    shard_count = lax.axis_size("fsdp")
    group_id = lax.axis_index("dp")
    shard_id = lax.axis_index("fsdp")
    token_total = jnp.sum(token_counts).astype(jnp.float32)
    valid_limit = jnp.sum(jnp.where(lax.iota(jnp.int32, group_count) == group_id, token_counts, 0))
    positions = shard_id * tok_dev + lax.iota(jnp.int32, tok_dev)
    row_keep = (positions < valid_limit).astype(jnp.bfloat16)[:, None]
    masked_acts = acts * row_keep
    masked_grads = out_grads * row_keep
    block_ids = shard_id * blocks_dev + lax.iota(jnp.int32, blocks_dev)
    border_keep = (block_ids > 0).astype(jnp.float32)[:, None, None]
    lead_k, lead_c = (
        spread(k_factor[0, :, :block_size], "fsdp", 0),
        spread(c_factor[0, :, :block_size], "fsdp", 0),
    )
    raw_acts, raw_grads = to_owners((masked_acts, masked_grads))
    lead_raw_acts, lead_raw_grads = fetch_lead((raw_acts, raw_grads))
    k_diag_half = k_factor[:, :, :block_size].astype(jnp.bfloat16)
    k_side_half = (k_factor[:, :, block_size:] * border_keep).astype(jnp.bfloat16)
    c_diag_half = c_factor[:, :, :block_size].astype(jnp.bfloat16)
    c_side_half = (c_factor[:, :, block_size:] * border_keep).astype(jnp.bfloat16)
    owned_acts = owner_image(raw_acts, lead_raw_acts, k_diag_half, k_side_half)
    owned_grads = owner_image(raw_grads, lead_raw_grads, c_diag_half, c_side_half)
    lead_acts = jnp.dot(
        lead_raw_acts, lead_k.astype(jnp.bfloat16), preferred_element_type=jnp.float32
    ).astype(jnp.bfloat16)
    lead_grads = jnp.dot(
        lead_raw_grads, lead_c.astype(jnp.bfloat16), preferred_element_type=jnp.float32
    ).astype(jnp.bfloat16)
    own_k, cross_k = block_stats(owned_acts, lead_acts, blocks_dev, block_size)
    own_c, cross_c = block_stats(owned_grads, lead_grads, blocks_dev, block_size)
    summed = lax.psum((own_k, cross_k, own_c, cross_c), "dp")
    gram_k = gram_trace(k_factor, border_keep)
    gram_c = gram_trace(c_factor, border_keep)
    local_traces = jnp.stack(
        [
            jnp.sum(jnp.trace(summed[0], axis1=1, axis2=2)),
            jnp.sum(jnp.trace(summed[2], axis1=1, axis2=2)),
            gram_k,
            gram_c,
        ]
    )
    totals = lax.psum(local_traces, "fsdp")
    trace_hk = totals[0] / token_total
    trace_hc = totals[1] / token_total
    scale_width = float(width)
    k_factor_new, k_moment_new = advance(
        k_factor,
        k_moment,
        summed[0] / token_total,
        summed[1] / token_total,
        lead_k,
        border_keep,
        trace_hc,
        totals[3],
        scale_width,
    )
    c_factor_new, c_moment_new = advance(
        c_factor,
        c_moment,
        summed[2] / token_total,
        summed[3] / token_total,
        lead_c,
        border_keep,
        trace_hk,
        totals[2],
        scale_width,
    )
    grad_rows = grad_weight.shape[0]
    grad_lead = spread(grad_weight, "fsdp", 0)
    k_diag = k_factor_new[:, :, :block_size].astype(jnp.bfloat16)
    k_side = k_factor_new[:, :, block_size:].astype(jnp.bfloat16)
    grad_blocked = grad_weight.reshape(grad_rows, blocks_dev, block_size)
    first_sum = jnp.einsum("rnk,nkj->rnj", grad_blocked, k_diag, preferred_element_type=jnp.float32)
    first_sum = first_sum + jnp.einsum(
        "rk,nkj->rnj", grad_lead, k_side, preferred_element_type=jnp.float32
    )
    first_product = first_sum.astype(jnp.bfloat16)
    own_second = jnp.einsum(
        "rnk,njk->rnj", first_product, k_diag, preferred_element_type=jnp.float32
    )
    lead_term = jnp.einsum("rnk,njk->rj", first_product, k_side, preferred_element_type=jnp.float32)
    lead_sum = lax.psum(lead_term, "fsdp")
    lead_mask = (block_ids == 0).astype(jnp.float32)[None, :, None]
    second_product = (own_second + lead_mask * lead_sum[:, None, :]).astype(jnp.bfloat16)
    row_blocks = grad_rows // block_size
    owner_count = shard_count // group_count
    c_half = c_factor_new.astype(jnp.bfloat16)
    fetched = []
    for owner_step in range(owner_count):
        fetched.append(spread(c_half, "fsdp", group_id * owner_count + owner_step))
    row_factor = jnp.concatenate(fetched, axis=0)
    c_diag = row_factor[:, :, :block_size]
    c_side = row_factor[:, :, block_size:]
    by_rows = second_product.reshape(row_blocks, block_size, blocks_dev * block_size)
    lead_rows = spread(by_rows[0], "dp", 0)
    third_sum = jnp.einsum("nki,nkc->nic", c_diag, by_rows, preferred_element_type=jnp.float32)
    third_sum = third_sum + jnp.einsum(
        "nki,kc->nic", c_side, lead_rows, preferred_element_type=jnp.float32
    )
    third_product = third_sum.astype(jnp.bfloat16)
    own_fourth = jnp.einsum(
        "nik,nkc->nic", c_diag, third_product, preferred_element_type=jnp.float32
    )
    row_term = jnp.einsum("nik,nkc->ic", c_side, third_product, preferred_element_type=jnp.float32)
    row_sum = lax.psum(row_term, "dp")
    row_ids = group_id * row_blocks + lax.iota(jnp.int32, row_blocks)
    row_mask = (row_ids == 0).astype(jnp.float32)[:, None, None]
    precond = (
        (own_fourth + row_mask * row_sum[None, :, :])
        .astype(jnp.bfloat16)
        .reshape(grad_rows, blocks_dev * block_size)
    )
    return (k_factor_new, c_factor_new, k_moment_new, c_moment_new, precond)


def solution(mesh):
    in_specs = (
        P(("dp", "fsdp"), None),
        P(("dp", "fsdp"), None),
        P(),
        P("fsdp", None, None),
        P("fsdp", None, None),
        P("fsdp", None, None),
        P("fsdp", None, None),
        P("dp", "fsdp"),
    )
    out_specs = (
        P("fsdp", None, None),
        P("fsdp", None, None),
        P("fsdp", None, None),
        P("fsdp", None, None),
        P("dp", "fsdp"),
    )
    return jax.shard_map(
        per_device, mesh=mesh, in_specs=in_specs, out_specs=out_specs, check_vma=False
    )
```

profile of v0, /device:TPU:0, one launch (start us, length us, event | category | flops | bytes accessed | tf_op | source)
XLA Modules:
  0.0 1121.6 jit_solution(17236621466288324182)
XLA Ops:
  7.2 3.2 copy.59
  10.4 4.1 copy.62
  15.9 3.2 broadcast_multiply_fusion.1
  19.1 60.6 %all_to_all.32 = bf16[128,32,256]{0,2,1:T(8,128)(2,1)} all-to-all(bf16[128,32,256]{0,2,1:T(8,128)(2,1)S(1)} %bitcast.259), channel_id=1, replica_groups=mesh['dp'=8,'fsdp'=32] {'fsdp'}, dimensions={1} | all-to-all | bytes 4194304 | tf_op jit(solution)/shard_map/all_to_all | solution.py:31
  79.7 5.3 all-to-all-start.1
  85.9 3.3 copy.60
  89.2 45.5 %all-to-all-done.1 = bf16[128,32,256]{0,2,1:T(8,128)(2,1)} async-done(((bf16[128,32,256]{0,2,1:T(8,128)(2,1)}), bf16[128,32,256]{0,2,1:T(8,128)(2,1)}, u32[]{:S(2)}, u32[]{:S(2)}) %all-to-all-start.1) | async-done | bytes 2097184 | tf_op jit(solution)/shard_map/all_to_all | solution.py:32
  134.7 4.1 copy.63
  138.8 3.9 broadcast_select_fusion
  145.9 162.0 %all-reduce.27.cloned.1.call-done = (bf16[4096,256]{1,0:T(8,128)(2,1)}, bf16[4096,256]{1,0:T(8,128)(2,1)}, bf16[1024,256]{1,0:T(8,128)(2,1)}) async-done(((bf16[4096,256]{1,0:T(8,128)(2,1)}, bf16[4096,256]{1,0:T(8,128)(2,1)}, bf16[1024,256]{1,0:T(8,128)(2,1)}), (bf16[4096,256]{1,0:T(8,128)(2,1)}, bf16[4096,256]{1,0:T(8,128)(2,1)}, bf16[1024,256]{1,0:T(8,128)(2,1)})) %all-reduce.27.cloned.1.call-update) | async-done | bytes 4718608 | tf_op jit(solution)/shard_map/psum | solution.py:14
  307.9 2.3 convolution_bitcast_fusion.2
  310.9 1.4 convolution_bitcast_fusion.13
  317.2 1.7 convolution_bitcast_fusion.12
  318.8 136.2 %all-reduce.13.cloned.1.call-done = f32[256,256]{1,0:T(8,128)} async-done(((f32[256,256]{1,0:T(8,128)}), f32[256,256]{1,0:T(8,128)}) %all-reduce.13.cloned.1.call-update) | async-done | bytes 262160 | tf_op jit(solution)/shard_map/psum | solution.py:14
  455.0 4.4 fusion.24
  464.8 58.7 %all-reduce.23.cloned.1.call-done = (f32[1,256,256]{1,2,0:T(8,128)}, f32[1,256,256]{2,1,0:T(8,128)}, f32[1,256,256]{2,1,0:T(8,128)}) async-done(((f32[1,256,256]{1,2,0:T(8,128)}, f32[1,256,256]{2,1,0:T(8,128)}, f32[1,256,256]{2,1,0:T(8,128)}), (f32[1,256,256]{1,2,0:T(8,128)}, f32[1,256,256]{2,1,0:T(8,128)}, f32[1,256,256]{2,1,0:T(8,128)})) %all-reduce.23.cloned.1.call-update) | async-done | bytes 786448 | tf_op jit(solution)/shard_map/psum | solution.py:118
  523.6 1.8 copy.61
  525.3 1.6 select_reduce_fusion.1
  526.9 1.6 select_reduce_fusion
  529.9 1.8 copy.66
  531.7 75.2 %psum.123 = f32[4]{0:T(128)S(1)} all-reduce(f32[4]{0:T(128)S(1)} %pad_maximum_fusion.4), channel_id=1, replica_groups=mesh['dp'=8,'fsdp'=32] {'fsdp'}, use_global_device_ids=true, to_apply=%region_11.12 | all-reduce | flops 4 | bytes 32 | tf_op jit(solution)/shard_map/psum | solution.py:129
  619.5 2.3 fusion.46
  621.8 1.8 copy.73
  626.5 133.2 %all-reduce.21.cloned.1.call-done = (f32[256,256]{1,0:T(8,128)}, f32[1024,256]{0,1:T(8,128)}) async-done(((f32[256,256]{1,0:T(8,128)}, f32[1024,256]{0,1:T(8,128)}), (f32[256,256]{1,0:T(8,128)}, f32[1024,256]{0,1:T(8,128)})) %all-reduce.21.cloned.1.call-update) | async-done | bytes 1310736 | tf_op jit(solution)/shard_map/psum | solution.py:14
  759.7 3.8 fusion.23
  764.9 61.5 %all-reduce.15.cloned.1.call-done = f32[1,256,256]{2,1,0:T(8,128)} async-done(((f32[1,256,256]{2,1,0:T(8,128)}), f32[1,256,256]{2,1,0:T(8,128)}) %all-reduce.15.cloned.1.call-update) | async-done | bytes 262160 | tf_op jit(solution)/shard_map/psum | solution.py:118
  826.4 1.7 fusion.34
  833.4 147.5 %all-reduce.25.cloned.1.call-done = (bf16[1,256,512]{2,1,0:T(8,128)(2,1)}, bf16[1,256,512]{2,1,0:T(8,128)(2,1)}, bf16[1,256,512]{2,1,0:T(8,128)(2,1)}, bf16[1,256,512]{2,1,0:T(8,128)(2,1)}) async-done(((bf16[1,256,512]{2,1,0:T(8,128)(2,1)}, bf16[1,256,512]{2,1,0:T(8,128)(2,1)}, bf16[1,256,512]{2,1,0:T(8,128)(2,1)}, bf16[1,256,512]{2,1,0:T(8,128)(2,1)}), (bf16[1,256,512]{2,1,0:T(8,128)(2,1)}, ...) | async-done | bytes 1048592 | tf_op jit(solution)/shard_map/psum | solution.py:14
  985.1 60.6 %all-reduce.17.cloned.1.call-done = bf16[256,256]{0,1:T(8,128)(2,1)} async-done(((bf16[256,256]{0,1:T(8,128)(2,1)}), bf16[256,256]{0,1:T(8,128)(2,1)}) %all-reduce.17.cloned.1.call-update) | async-done | bytes 131088 | tf_op jit(solution)/shard_map/psum | solution.py:14
  1048.9 1.8 pad_maximum_fusion.3
  1050.7 62.0 %all-reduce.19.cloned.1.call-done = f32[256,256]{1,0:T(8,128)} async-done(((f32[256,256]{1,0:T(8,128)}), f32[256,256]{1,0:T(8,128)}) %all-reduce.19.cloned.1.call-update) | async-done | bytes 262160 | tf_op jit(solution)/shard_map/psum | solution.py:192
  1112.7 2.0 fusion.13
  (110 shorter events, 41.0 us)
Async XLA Ops:
  10.4 4.1 copy-start.23
  79.7 5.4 copy-start.12
  79.7 55.0 %all-to-all-start.1 = ((bf16[128,32,256]{0,2,1:T(8,128)(2,1)}), bf16[128,32,256]{0,2,1:T(8,128)(2,1)}, u32[]{:S(2)}, u32[]{:S(2)}) async-start(bf16[128,32,256]{0,2,1:T(8,128)(2,1)} %bitcast.12), calls=%async_computation.1 | async-start | bytes 4194304 | tf_op jit(solution)/shard_map/all_to_all | solution.py:32
  85.0 222.9 %all-reduce.27.cloned.1.call-start = ((), (), s32[]{:S(2)}) async-start(), calls=%async_computation.9 | async-start | bytes 9437184 | tf_op jit(solution)/shard_map/psum | solution.py:14
  142.7 1.0 copy-start.1
  142.7 312.3 %all-reduce.13.cloned.1.call-start = ((), (), s32[]{:S(2)}) async-start(), calls=%async_computation.2 | async-start | bytes 524288 | tf_op jit(solution)/shard_map/psum | solution.py:14
  144.5 379.1 %all-reduce.23.cloned.1.call-start = ((), (), s32[]{:S(2)}) async-start(), calls=%async_computation.7 | async-start | bytes 1572864 | tf_op jit(solution)/shard_map/psum | solution.py:118
  310.9 1.5 copy-start.11
  310.9 1.5 copy-start.2
  310.9 2.6 copy-start.3
  313.5 1.6 copy-start
  315.8 1.3 copy-start.10
  459.4 300.3 %all-reduce.21.cloned.1.call-start = ((), (), s32[]{:S(2)}) async-start(), calls=%async_computation.6 | async-start | bytes 2621440 | tf_op jit(solution)/shard_map/psum | solution.py:14
  611.2 2.1 copy-start.20
  611.2 2.1 copy-start.22
  611.3 2.1 copy-start.24
  612.5 1.9 copy-start.8
  612.5 2.2 copy-start.19
  613.4 1.7 copy-start.13
  614.0 0.7 copy-start.15
  614.7 0.7 copy-start.4
  616.8 209.6 %all-reduce.15.cloned.1.call-start = ((), (), s32[]{:S(2)}) async-start(), calls=%async_computation.3 | async-start | bytes 524288 | tf_op jit(solution)/shard_map/psum | solution.py:118
  763.5 65.4 %copy-start.21 = (f32[256,256]{1,0:T(8,128)S(1)}, f32[256,256]{1,0:T(8,128)}, u32[]{:S(2)}) copy-start(f32[256,256]{1,0:T(8,128)} %get-tuple-element.11) | copy-start | bytes 786436
  763.5 65.8 %copy-start.18 = (f32[1,256,256]{2,1,0:T(8,128)S(1)}, f32[1,256,256]{2,1,0:T(8,128)}, u32[]{:S(2)}) copy-start(f32[1,256,256]{2,1,0:T(8,128)} %fusion.40) | copy-start | bytes 786436
  763.5 217.4 %all-reduce.25.cloned.1.call-start = ((), (), s32[]{:S(2)}) async-start(), calls=%async_computation.8 | async-start | bytes 2097152 | tf_op jit(solution)/shard_map/psum | solution.py:14
  829.2 2.0 copy-start.9
  829.3 2.0 copy-start.16
  829.3 2.9 copy-start.14
  831.2 214.6 %all-reduce.17.cloned.1.call-start = ((), (), s32[]{:S(2)}) async-start(), calls=%async_computation.4 | async-start | bytes 262144 | tf_op jit(solution)/shard_map/psum | solution.py:14
  833.4 279.3 %all-reduce.19.cloned.1.call-start = ((), (), s32[]{:S(2)}) async-start(), calls=%async_computation.5 | async-start | bytes 524288 | tf_op jit(solution)/shard_map/psum | solution.py:192
  985.1 62.9 %copy-start.5 = (f32[1,256,256]{2,1,0:T(8,128)S(1)}, f32[1,256,256]{2,1,0:T(8,128)}, u32[]{:S(2)}) copy-start(f32[1,256,256]{2,1,0:T(8,128)} %copy-done.4) | copy-start | bytes 786436
  985.1 63.8 %copy-start.7 = (f32[1,256,256]{2,1,0:T(8,128)S(1)}, f32[1,256,256]{2,1,0:T(8,128)}, u32[]{:S(2)}) copy-start(f32[1,256,256]{2,1,0:T(8,128)} %copy-done.6) | copy-start | bytes 786436
  (2 other events, 1.4 us)
Sparse Core Ops, SparseCore 0:
  142.8 165.0 all-reduce.26
  311.9 143.0 all-reduce.12
  459.5 63.9 all-reduce.22
  616.9 142.7 all-reduce.20
  763.6 62.7 all-reduce.14
  831.3 149.5 all-reduce.24
  983.2 62.5 all-reduce.16
  1048.2 64.4 all-reduce.18
where the time goes:
time: 1120 us
  waiting for transfers between devices  867 us (77%)
  blocking collectives  136 us (12%)
  matrix products  34.6 us (3%)
  local copies, waits for them, and re-layouts  31.9 us (3%)
  other arithmetic  25.8 us (2%)
  between operations  20.5 us (2%)
    psum x5, waiting for transfers between devices, spread(): return lax.psum(kept, axis)  639 us
    psum x2, waiting for transfers between devices, per_device(): summed = lax.psum((own_k, cross_k, own_c, cross_c), 'dp')  120 us
    psum x1, blocking collectives, per_device(): totals = lax.psum(local_traces, 'fsdp')  75.2 us
    psum x1, waiting for transfers between devices, per_device(): row_sum = lax.psum(row_term, 'dp')  62 us
    all_to_all x1, blocking collectives, to_owners(): lax.all_to_all(pair[0], 'fsdp', split_axis=1, concat_axis=0, tiled=True)  60.6 us
    all_to_all x1, waiting for transfers between devices, to_owners(): lax.all_to_all(pair[1], 'fsdp', split_axis=1, concat_axis=0, tiled=True)  45.5 us
  transfers between devices with their start and end apart: 9, of which 9 were waited for; matrix products, arithmetic and copies ran while one was open for 3% of the time, Pallas kernels for 0%

commit v1 on v0

v1 whole, which is shorter than its diff:
```python
import functools

import jax
import jax.numpy as jnp
from jax import lax
from jax.experimental import pallas as pl
from jax.experimental.pallas import tpu as pltpu
from jax.sharding import PartitionSpec as P

MESH = pl.DeviceIdType.MESH
highest = lax.Precision.HIGHEST
f32 = jnp.float32
bf16 = jnp.bfloat16

damping = 0.1
momentum_rate = 0.5
step_rate = 0.2

NX, NY, NZ = 4, 4, 8


def position():
    d = lax.axis_index("dp")
    f = lax.axis_index("fsdp")
    return lax.div(f, NZ), lax.div(d, 2), lax.rem(f, NZ), lax.rem(d, 2)


def device(x, y, z, c):
    return (y * 2 + c, x * NZ + z)


def class_of(x, y, z, c):
    return lax.rem(x, 2) * 8 + lax.rem(y, 2) * 4 + c * 2 + lax.rem(z, 2)


def send(src, dst, send_sem, recv_sem, target):
    return pltpu.make_async_remote_copy(
        src_ref=src, dst_ref=dst, send_sem=send_sem, recv_sem=recv_sem, device_id=target, device_id_type=MESH
    )


def arrived(dst, sem):
    pltpu.make_async_copy(dst, dst, sem).wait()


def greet(barrier, target):
    pl.semaphore_signal(barrier, inc=1, device_id=target, device_id_type=MESH)


ANY = pl.BlockSpec(memory_space=pl.ANY)
VM = pl.BlockSpec(memory_space=pltpu.VMEM)
DMA = pltpu.SemaphoreType.DMA


def call(body, name, ins, in_specs, outs, out_specs, scratch=(), cid=None):
    params = dict(collective_id=cid, has_side_effects=True) if cid is not None else {}
    return pl.pallas_call(
        body,
        out_shape=[jax.ShapeDtypeStruct(s, t) for s, t in outs],
        in_specs=in_specs,
        out_specs=out_specs,
        scratch_shapes=list(scratch),
        compiler_params=pltpu.CompilerParams(**params),
        name=name,
    )(*ins)


def token_body(acts, grads, keep, pieces, xc, x0, piece, xs, ls, s1, r1, s2, r2, s3, r3, l1, l2):
    x, y, z, c = position()
    d, f = lax.axis_index("dp"), lax.axis_index("fsdp")
    barrier = pltpu.get_barrier_semaphore()

    def at(sign, a, b, g, e):
        return (
            lax.rem(x + sign * a + NX, NX),
            lax.rem(y + sign * b + NY, NY),
            lax.rem(z + sign * g + NZ, NZ),
            lax.rem(c + e, 2),
        )

    offsets = [(a, b, g, e) for a in (0, 1) for b in (0, 1) for g in (0, 1) for e in (0, 1)]
    for sign in (1, -1):
        for o in offsets:
            if o[:3] == (0, 0, 0) and (o[3] == 0 or sign == -1):
                continue
            greet(barrier, device(*at(sign, *o)))

    @pl.when(f > 0)
    def _():
        greet(barrier, (d, 0))

    for side, ref in enumerate((acts, grads)):
        for h in range(2):
            rows = slice(h * 64, h * 64 + 64)
            kept = keep[rows, :]
            ls[h, side, :, :] = ref[rows, 0:256] * kept
            for k in range(16):
                for m in range(2):
                    n = m * 16 + k
                    xs[k, h, side, :, m * 256 : m * 256 + 256] = ref[rows, n * 256 : n * 256 + 256] * kept

    pl.semaphore_wait(barrier, 29 + jnp.where(f == 0, 31, 0))
    copies = []
    for h, sign in ((0, 1), (1, -1)):
        for i, o in enumerate(offsets):
            there = at(sign, *o)
            k = class_of(*there)
            slot = h * 16 + i
            if i == 0:
                one = pltpu.make_async_copy(xs.at[k, h], xc.at[:, slot], l1.at[h])
                two = pltpu.make_async_copy(ls.at[h], x0.at[:, slot], l2.at[h])
            else:
                one = send(xs.at[k, h], xc.at[:, slot], s1.at[slot], r1.at[slot], device(*there))
                two = send(ls.at[h], x0.at[:, slot], s2.at[slot], r2.at[slot], device(*there))
            one.start()
            two.start()
            copies += [one, two]

    @pl.when(f == 0)
    def _():
        own = pltpu.make_async_copy(pieces.at[0], piece, r3)
        own.start()

        @pl.loop(1, 32)
        def _(t):
            send(pieces.at[t], piece, s3.at[t], r3, (d, t)).start()

        @pl.loop(1, 32)
        def _(t):
            send(pieces.at[t], piece, s3.at[t], r3, (d, t)).wait_send()

    arrived(piece, r3)
    for one in copies:
        one.wait()


def gram_body(xc, x0, out):
    dims = (((0,), (0,)), ((), ()))
    for side in range(2):
        lead = x0[side]
        a = xc[side, :, 0:256]
        b = xc[side, :, 256:512]
        for i, (l, r) in enumerate(((a, a), (b, b), (lead, a), (lead, b), (lead, lead))):
            g = lax.dot_general(l, r, dims, preferred_element_type=f32)
            out[:, side * 5 + i, :, :] = g.astype(bf16).reshape(16, 16, 256)


def scatter_body(parts, out, s, r, l):
    x, y, z, c = position()
    barrier = pltpu.get_barrier_semaphore()
    offsets = [(a, b, g) for a in range(2) for b in range(2) for g in range(4)]

    def at(a, b, g):
        return lax.rem(x + 2 * a, NX), lax.rem(y + 2 * b, NY), lax.rem(z + 2 * g, NZ)

    for o in offsets[1:]:
        greet(barrier, device(*at(*o), c))
    pl.semaphore_wait(barrier, 15)
    copies = []
    for i, o in enumerate(offsets):
        tx, ty, tz = at(*o)
        j = lax.div(tx, 2) * 8 + lax.div(ty, 2) * 4 + lax.div(tz, 2)
        if i == 0:
            copy = pltpu.make_async_copy(parts.at[j], out.at[0], l)
        else:
            copy = send(parts.at[j], out.at[i], s.at[i], r.at[i], device(tx, ty, tz, c))
        copy.start()
        copies.append(copy)
    for copy in copies:
        copy.wait()


def sum_body(parts, out):
    total = parts[0].astype(f32)
    for i in range(1, 16):
        total = total + parts[i].astype(f32)
    total = total.astype(bf16)
    for m in range(2):
        for side in range(2):
            for q, source in enumerate((m, 2 + m, 4)):
                out[m, side * 3 + q] = total[side * 5 + source]


def deliver_body(rows, out, s, r):
    x, y, z, c = position()
    d, f = lax.axis_index("dp"), lax.axis_index("fsdp")
    barrier = pltpu.get_barrier_semaphore()
    mine = class_of(x, y, z, c)
    slot = lax.div(x, 2) * 8 + lax.div(y, 2) * 4 + lax.div(z, 2)
    k = lax.rem(f, 16)
    px, py, pc, pz = lax.div(k, 8), lax.rem(lax.div(k, 4), 2), lax.rem(lax.div(k, 2), 2), lax.rem(k, 2)
    own = jnp.where(mine == k, 1, 0)

    def source(j):
        return device(px + 2 * lax.div(j, 8), py + 2 * lax.rem(lax.div(j, 4), 2), pz + 2 * lax.rem(j, 4), pc)

    def is_me(there):
        return jnp.logical_and(there[0] == d, there[1] == f)

    @pl.loop(0, 16)
    def _(j):
        there = source(j)

        @pl.when(jnp.logical_not(is_me(there)))
        def _():
            greet(barrier, there)

    pl.semaphore_wait(barrier, 16 - own)

    @pl.loop(0, 16)
    def _(t):
        m = lax.div(t, 8)
        there = (lax.rem(t, 8), mine + 16 * m)

        @pl.when(is_me(there))
        def _():
            pltpu.make_async_copy(rows.at[m], out.at[slot], r.at[slot]).start()

        @pl.when(jnp.logical_not(is_me(there)))
        def _():
            send(rows.at[m], out.at[slot], s.at[t], r.at[slot], there).start()

    @pl.loop(0, 16)
    def _(t):
        m = lax.div(t, 8)
        there = (lax.rem(t, 8), mine + 16 * m)

        @pl.when(jnp.logical_not(is_me(there)))
        def _():
            send(rows.at[m], out.at[slot], s.at[t], r.at[slot], there).wait_send()

    @pl.loop(0, 16)
    def _(j):
        arrived(out.at[j], r.at[j])


def dot(a, b):
    return jnp.dot(a, b, precision=highest, preferred_element_type=f32)


def dot16(a, b):
    return jnp.dot(a, b, preferred_element_type=f32)


def second_moment_body(stats, k_factor, c_factor, keep, u_out, h_out, tr_out):
    flag = keep[0:1, 0:1]
    rows = lax.broadcasted_iota(jnp.int32, (256, 256), 0)
    cols = lax.broadcasted_iota(jnp.int32, (256, 256), 1)
    for side, factor in enumerate((k_factor, c_factor)):
        a = stats[:, side * 3 + 0].reshape(256, 256)
        cross = stats[:, side * 3 + 1].reshape(256, 256)
        lead = stats[:, side * 3 + 2].reshape(256, 256)
        diag = factor[0, :, 0:256]
        border = factor[0, :, 256:512] * flag
        diag16, border16 = diag.astype(bf16), border.astype(bf16)
        u = dot16(cross, diag16) + dot16(lead, border16)
        v = dot16(a, diag16) + dot16(cross.T, border16)
        h = dot(diag16.astype(f32).T, v) + dot(border16.astype(f32).T, u)
        u_out[side] = u
        h_out[side] = h
        tr_h = jnp.sum(jnp.where(rows == cols, h, 0.0))
        tr_g = jnp.sum(diag * diag) + jnp.sum(border * border)
        tr_out[side * 2 : side * 2 + 1, :] = jnp.full((1, 128), tr_h, f32)
        tr_out[side * 2 + 1 : side * 2 + 2, :] = jnp.full((1, 128), tr_g, f32)
    tr_out[4:8, :] = jnp.zeros((4, 128), f32)


def gather_body(count, *refs):
    ins, outs, sems = refs[:count], refs[count : 2 * count], refs[2 * count :]
    d, f = lax.axis_index("dp"), lax.axis_index("fsdp")
    barrier = pltpu.get_barrier_semaphore()

    @pl.loop(1, 32)
    def _(t):
        greet(barrier, (d, lax.rem(f + t, 32)))

    pl.semaphore_wait(barrier, 31)
    for i in range(count):
        s, r = sems[2 * i], sems[2 * i + 1]
        pltpu.make_async_copy(ins[i], outs[i].at[f], r.at[0]).start()

        @pl.loop(1, 32)
        def _(t):
            send(ins[i], outs[i].at[f], s.at[t], r.at[t], (d, lax.rem(f + t, 32))).start()

    for i in range(count):
        s, r = sems[2 * i], sems[2 * i + 1]
        arrived(outs[i].at[f], r.at[0])

        @pl.loop(1, 32)
        def _(t):
            send(ins[i], outs[i].at[f], s.at[t], r.at[t], (d, lax.rem(f + t, 32))).wait_send()
            arrived(outs[i].at[lax.rem(f + 32 - t, 32)], r.at[t])


def gather(ins, cid, name):
    n = len(ins)
    return call(
        functools.partial(gather_body, n),
        name,
        ins,
        [ANY] * n,
        [((32,) + v.shape, v.dtype) for v in ins],
        [ANY] * n,
        [DMA((32,))] * (2 * n),
        cid,
    )


def advance_body(
    tr, total, keep, h_in, u_in, k_factor, c_factor, k_moment, c_moment, lead_pieces, grad, k_new, c_new, km_new, cm_new,
    c_half, own_out, lead_out,
):
    flag = keep[0:1, 0:1]
    inverse = 1.0 / total[0:1, 0:1]
    width = 8192.0
    sums = tr[0]
    for i in range(1, 32):
        sums = sums + tr[i]
    trace = [sums[i : i + 1, 0:1] for i in range(4)]
    rows = lax.broadcasted_iota(jnp.int32, (256, 256), 0)
    cols = lax.broadcasted_iota(jnp.int32, (256, 256), 1)
    identity = jnp.where(rows == cols, 1.0, 0.0)
    halves = []
    for side, (factor, moment, f_new, m_new) in enumerate(
        ((k_factor, k_moment, k_new, km_new), (c_factor, c_moment, c_new, cm_new))
    ):
        other_h = trace[2 - 2 * side] * inverse * inverse
        other_g = trace[3 - 2 * side] * damping
        diag = factor[0, :, 0:256]
        border = factor[0, :, 256:512] * flag
        lead = lead_pieces[:, side * 8 : side * 8 + 8].reshape(256, 256).astype(f32)
        gram = dot(diag.T, diag) + dot(border.T, border)
        fresh = (other_h * h_in[side] + other_g * gram - width * identity) / (2.0 * width)
        cross = dot(lead.T, other_h * u_in[side] + other_g * border) * flag / (2.0 * width)
        m_diag = momentum_rate * moment[0, :, 0:256] + fresh
        m_side = (momentum_rate * moment[0, :, 256:512] + cross) * flag
        n_diag = diag - step_rate * dot(diag, m_diag)
        n_side = (border - step_rate * (dot(lead, m_side) + dot(border, m_diag))) * flag
        f_new[0, :, 0:256] = n_diag
        f_new[0, :, 256:512] = n_side
        m_new[0, :, 0:256] = m_diag
        m_new[0, :, 256:512] = m_side
        halves.append((n_diag.astype(bf16), n_side.astype(bf16)))
    k_diag, k_side = halves[0]
    c_half[0:256, :] = halves[1][0]
    c_half[256:512, :] = halves[1][1]
    grad_lead = lead_pieces[:, 16:48].reshape(1024, 256)
    first = (dot16(grad[...], k_diag) + dot16(grad_lead, k_side)).astype(bf16)
    own_out[...] = dot16(first, k_diag.T)
    lead_out[...] = dot16(first, k_side.T).astype(bf16).reshape(32, 32, 256)


def border_body(lead, c_half, parts, c_part, s, r, s2, r2, l):
    d, f = lax.axis_index("dp"), lax.axis_index("fsdp")
    barrier = pltpu.get_barrier_semaphore()
    own = pltpu.make_async_copy(lead.at[f], parts.at[f], l)
    own.start()

    @pl.loop(1, 32)
    def _(t):
        greet(barrier, (d, lax.rem(f + t, 32)))

    pl.semaphore_wait(barrier, 31)
    root = lax.div(f, 4) == d
    q = lax.rem(f, 4)

    @pl.loop(1, 32)
    def _(t):
        there = lax.rem(f + t, 32)
        send(lead.at[there], parts.at[f], s.at[t], r.at[t], (d, there)).start()

    @pl.when(root)
    def _():
        pltpu.make_async_copy(c_half.at[pl.ds(pl.multiple_of(f * 16, 16), 16)], c_part.at[q], r2.at[q]).start()

        @pl.loop(1, 32)
        def _(t):
            there = lax.rem(f + t, 32)
            src = c_half.at[pl.ds(pl.multiple_of(there * 16, 16), 16)]
            send(src, c_part.at[q], s2.at[t], r2.at[q], (d, there)).start()

    own.wait()

    @pl.loop(1, 32)
    def _(t):
        there = lax.rem(f + t, 32)
        send(lead.at[there], parts.at[f], s.at[t], r.at[t], (d, there)).wait_send()
        arrived(parts.at[lax.rem(f + 32 - t, 32)], r.at[t])

    @pl.when(root)
    def _():
        @pl.loop(1, 32)
        def _(t):
            there = lax.rem(f + t, 32)
            src = c_half.at[pl.ds(pl.multiple_of(there * 16, 16), 16)]
            send(src, c_part.at[q], s2.at[t], r2.at[q], (d, there)).wait_send()

    for j in range(4):
        arrived(c_part.at[j], r2.at[j])


def border_sum_body(parts, out):
    total = parts[0].astype(f32)
    for i in range(1, 32):
        total = total + parts[i].astype(f32)
    out[...] = total.astype(bf16)


def factors_body(c_part, lead, all_c, all_lead, s, r, s2, r2):
    d, f = lax.axis_index("dp"), lax.axis_index("fsdp")
    barrier = pltpu.get_barrier_semaphore()

    @pl.loop(1, 32)
    def _(t):
        greet(barrier, (d, lax.rem(f + t, 32)))

    pl.semaphore_wait(barrier, 31)

    @pl.when(f > 0)
    def _():
        send(lead, all_lead.at[f], s2, r2.at[f], (d, 0)).start()

    @pl.when(f == 0)
    def _():
        pltpu.make_async_copy(lead, all_lead.at[0], r2.at[0]).start()

    pltpu.make_async_copy(c_part, all_c.at[f], r.at[0]).start()

    @pl.loop(1, 32)
    def _(t):
        send(c_part, all_c.at[f], s.at[t], r.at[t], (d, lax.rem(f + t, 32))).start()

    arrived(all_c.at[f], r.at[0])

    @pl.loop(1, 32)
    def _(t):
        send(c_part, all_c.at[f], s.at[t], r.at[t], (d, lax.rem(f + t, 32))).wait_send()
        arrived(all_c.at[lax.rem(f + 32 - t, 32)], r.at[t])

    @pl.when(f > 0)
    def _():
        send(lead, all_lead.at[f], s2, r2.at[f], (d, 0)).wait_send()

    @pl.when(f == 0)
    def _():
        @pl.loop(0, 32)
        def _(t):
            arrived(all_lead.at[t], r2.at[t])


def second_body(first_flag, own, lead, out):
    kept = jnp.where(first_flag[0:1, 0:1] > 0.0, lead[...].reshape(1024, 256).astype(f32), 0.0)
    out[...] = (own[...] + kept).astype(bf16)


def rows_body(second, out, s, r):
    d, f = lax.axis_index("dp"), lax.axis_index("fsdp")
    barrier = pltpu.get_barrier_semaphore()
    src = second.at[0:256]

    @pl.when(d > 0)
    def _():
        greet(barrier, (0, f))
        arrived(out, r)

    @pl.when(d == 0)
    def _():
        pl.semaphore_wait(barrier, 7)
        pltpu.make_async_copy(src, out, r).start()
        for t in range(1, 8):
            send(src, out, s.at[t], r, (t, f)).start()
        arrived(out, r)
        for t in range(1, 8):
            send(src, out, s.at[t], r, (t, f)).wait_send()


def third_body(second, lead_rows, pieces, own_out, term_out):
    term = jnp.zeros((256, 256), f32)
    for j in range(4):
        diag = pieces[0:16, j].reshape(256, 256)
        side = pieces[16:32, j].reshape(256, 256)
        third = dot16(diag.T, second[j * 256 : j * 256 + 256, :]) + dot16(side.T, lead_rows[...])
        third = third.astype(bf16)
        own_out[j * 256 : j * 256 + 256, :] = dot16(diag, third)
        term = term + dot16(side, third)
    term_out[...] = term.astype(bf16)


def term_body(term, out, s, r, l):
    d, f = lax.axis_index("dp"), lax.axis_index("fsdp")
    barrier = pltpu.get_barrier_semaphore()

    @pl.when(d > 0)
    def _():
        pl.semaphore_wait(barrier, 1)
        copy = send(term, out.at[d], s, r.at[d], (0, f))
        copy.start()
        copy.wait_send()

    @pl.when(d == 0)
    def _():
        for t in range(1, 8):
            greet(barrier, (t, f))
        own = pltpu.make_async_copy(term, out.at[0], l)
        own.start()
        own.wait()
        for t in range(1, 8):
            arrived(out.at[t], r.at[t])


def final_body(flag, own, terms, out):
    total = jnp.zeros((256, 256), f32)
    kept = flag[0:1, 0:1] > 0.0
    for i in range(8):
        total = total + terms[i].astype(f32)
    out[0:256, :] = (own[0:256, :] + jnp.where(kept, total, 0.0)).astype(bf16)
    out[256:1024, :] = own[256:1024, :].astype(bf16)


def per_device(acts, out_grads, token_counts, k_factor, c_factor, k_moment, c_moment, grad_weight):
    d = lax.axis_index("dp")
    f = lax.axis_index("fsdp")
    token_total = jnp.broadcast_to(jnp.sum(token_counts).astype(f32), (8, 128))
    limit = jnp.sum(jnp.where(lax.iota(jnp.int32, 8) == d, token_counts, 0))
    keep = (f * 128 + lax.broadcasted_iota(jnp.int32, (128, 256), 0) < limit).astype(bf16)
    border_keep = jnp.broadcast_to((f > 0).astype(f32), (8, 128))
    first_column = jnp.broadcast_to((f == 0).astype(f32), (8, 128))
    first_row = jnp.broadcast_to((d == 0).astype(f32), (8, 128))
    pieces = jnp.concatenate(
        [
            k_factor[0, :, :256].astype(bf16).reshape(32, 8, 256),
            c_factor[0, :, :256].astype(bf16).reshape(32, 8, 256),
            grad_weight.reshape(32, 32, 256),
        ],
        axis=1,
    )
    xc, x0, piece = call(
        token_body, "tokens", (acts, out_grads, keep, pieces), [VM, VM, VM, ANY],
        [((2, 32, 64, 512), bf16), ((2, 32, 64, 256), bf16), ((48, 256), bf16)], [ANY, ANY, ANY],
        [pltpu.VMEM((16, 2, 2, 64, 512), bf16), pltpu.VMEM((2, 2, 64, 256), bf16)]
        + [DMA((32,))] * 4 + [DMA((32,)), DMA, DMA((2,)), DMA((2,))],
        0,
    )
    (parts,) = call(
        gram_body, "gram", (xc.reshape(2, 2048, 512), x0.reshape(2, 2048, 256)), [VM, VM],
        [((16, 10, 16, 256), bf16)], [VM],
    )
    (shares,) = call(
        scatter_body, "scatter", (parts,), [ANY], [((16, 10, 16, 256), bf16)], [ANY], [DMA((16,)), DMA((16,)), DMA], 1
    )
    (rows,) = call(sum_body, "sum", (shares,), [VM], [((2, 6, 16, 256), bf16)], [VM])
    (stats,) = call(
        deliver_body, "deliver", (rows,), [ANY], [((16, 6, 16, 256), bf16)], [ANY], [DMA((16,)), DMA((16,))], 2
    )
    u, h, traces = call(
        second_moment_body, "moments", (stats, k_factor, c_factor, border_keep), [VM] * 4,
        [((2, 256, 256), f32), ((2, 256, 256), f32), ((8, 128), f32)], [VM] * 3,
    )
    all_traces, lead_pieces = gather((traces, piece), 3, "traces")
    k_new, c_new, km_new, cm_new, c_half, own_second, lead_term = call(
        advance_body, "advance",
        (all_traces, token_total, border_keep, h, u, k_factor, c_factor, k_moment, c_moment, lead_pieces, grad_weight),
        [VM] * 11,
        [((1, 256, 512), f32)] * 4
        + [((512, 256), bf16), ((1024, 256), f32), ((32, 32, 256), bf16)],
        [VM] * 7,
    )
    lead_parts, c_part = call(
        border_body, "border", (lead_term, c_half), [ANY, ANY],
        [((32, 32, 256), bf16), ((4, 16, 256), bf16)], [ANY, ANY],
        [DMA((32,)), DMA((32,)), DMA((32,)), DMA((4,)), DMA], 4,
    )
    (lead_rows32,) = call(border_sum_body, "border_sum", (lead_parts,), [VM], [((32, 256), bf16)], [VM])
    all_c, all_lead = call(
        factors_body, "factors", (c_part, lead_rows32), [ANY, ANY],
        [((32, 4, 16, 256), bf16), ((32, 32, 256), bf16)], [ANY, ANY],
        [DMA((32,)), DMA((32,)), DMA, DMA((32,))], 5,
    )
    (second,) = call(
        second_body, "second", (first_column, own_second, all_lead), [VM] * 3, [((1024, 256), bf16)], [VM]
    )
    (lead_rows,) = call(
        rows_body, "rows", (second,), [ANY], [((256, 256), bf16)], [ANY], [DMA((8,)), DMA], 6
    )
    own_fourth, term = call(
        third_body, "third", (second, lead_rows, all_c), [VM] * 3,
        [((1024, 256), f32), ((256, 256), bf16)], [VM] * 2,
    )
    (terms,) = call(
        term_body, "terms", (term,), [ANY], [((8, 256, 256), bf16)], [ANY], [DMA, DMA((8,)), DMA], 7
    )
    (precond,) = call(final_body, "final", (first_row, own_fourth, terms), [VM] * 3, [((1024, 256), bf16)], [VM])
    return k_new, c_new, km_new, cm_new, precond


def solution(mesh):
    in_specs = (
        P(("dp", "fsdp"), None),
        P(("dp", "fsdp"), None),
        P(),
        P("fsdp", None, None),
        P("fsdp", None, None),
        P("fsdp", None, None),
        P("fsdp", None, None),
        P("dp", "fsdp"),
    )
    out_specs = (
        P("fsdp", None, None),
        P("fsdp", None, None),
        P("fsdp", None, None),
        P("fsdp", None, None),
        P("dp", "fsdp"),
    )
    return jax.shard_map(per_device, mesh=mesh, in_specs=in_specs, out_specs=out_specs, check_vma=False)
```

time: 1120 us -> 285 us (0.25)
  waiting for transfers between devices: 867 us -> 0 us
  Pallas kernels: 0 us -> 274 us
  blocking collectives: 136 us -> 0 us
  matrix products: 34.6 us -> 0 us
  local copies, waits for them, and re-layouts: 31.9 us -> 4.15 us
  other arithmetic: 25.8 us -> 3.92 us
  between operations: 20.5 us -> 1.38 us
    psum x8 -> x0, waiting for transfers between devices: 822 us -> none  [the longest x5 639 us: spread(): return lax.psum(kept, axis)]
    pallas_call x0 -> x16, Pallas kernels: none -> 274 us  [call(): pl.pallas_call(body, out_shape=[jax.ShapeDtypeStruct(s, t) for s, t in ou...]
    psum x1 -> x0, blocking collectives: 75.2 us -> none  [per_device(): totals = lax.psum(local_traces, 'fsdp')]
    all_to_all x1 -> x0, blocking collectives: 60.6 us -> none  [to_owners(): lax.all_to_all(pair[0], 'fsdp', split_axis=1, concat_axis=0, tiled=True)]
    all_to_all x1 -> x0, waiting for transfers between devices: 45.5 us -> none  [to_owners(): lax.all_to_all(pair[1], 'fsdp', split_axis=1, concat_axis=0, tiled=True)]
    dot_general x28 -> x0, matrix products: 34.6 us -> none  [the longest x2 8.14 us: block_stats(): jnp.einsum('ti,tnj->nij', lead_image, blocked, preferred_element_type=jnp...]
    unnamed x55 -> x0, local copies, waits for them, and re-layouts: 16.3 us -> none
  transfers between devices with their start and end apart: 9 -> 0, of which waited for: 9 -> 0; matrix products, arithmetic and copies ran while one was open for 3% -> 0% of each run, Pallas kernels for 0% -> 0%
where the time goes in v1:
time: 285 us; the launch traced here: 284 us
  Pallas kernels  274 us (96%)
  local copies, waits for them, and re-layouts  4.15 us (1%)
  other arithmetic  3.92 us (1%)
    pallas_call x16, Pallas kernels, call(): pl.pallas_call(body, out_shape=[jax.ShapeDtypeStruct(s, t) for s, t in ou...  274 us

profile of v1, /device:TPU:0, one launch (start us, length us, event | category | flops | bytes accessed | tf_op | source)
XLA Modules:
  0.0 283.6 jit_solution(13283054996592482215)
XLA Ops:
  0.6 1.3 fusion.3
  1.9 0.6 compare_convert_fusion
  2.6 0.7 iota.11.keep
  3.3 1.1 fusion
  4.4 2.0 pad_maximum_fusion.pieces
  6.3 59.1 %tokens.1 = (bf16[2,32,64,512]{3,2,1,0:T(8,128)(2,1)}, bf16[2,32,64,256]{3,2,1,0:T(8,128)(2,1)}, bf16[48,256]{1,0:T(8,128)(2,1)}) custom-call(bf16[128,8192]{1,0:T(8,128)(2,1)} %acts.1, bf16[128,8192]{1,0:T(8,128)(2,1)} %grads.1, bf16[128,256]{1,0:T(8,128)(2,1)} %iota.11.keep, bf16[32,48,256]{2,1,0:T(8,128)(2,1)} %pad_maximum_fusion.pieces), custom_call_target="tpu_custom_call" | custom-call | tf_op jit(solution)/shard_map/tokens/pallas_call | solution.py:57
  65.5 6.9 %gram.1.parts = bf16[16,10,16,256]{3,2,1,0:T(8,128)(2,1)} custom-call(bf16[2,2048,512]{2,1,0:T(8,128)(2,1)} %bitcast.7, bf16[2,2048,256]{2,1,0:T(8,128)(2,1)} %bitcast.9), custom_call_target="tpu_custom_call" | custom-call | tf_op jit(solution)/shard_map/gram/pallas_call | solution.py:57
  72.4 39.5 %scatter.1.parts = bf16[16,10,16,256]{3,2,1,0:T(8,128)(2,1)} custom-call(bf16[16,10,16,256]{3,2,1,0:T(8,128)(2,1)} %gram.1.parts), custom_call_target="tpu_custom_call" | custom-call | tf_op jit(solution)/shard_map/scatter/pallas_call | solution.py:57
  111.9 2.1 sum.1.rows
  114.0 15.3 %deliver.1.stats = bf16[16,6,16,256]{3,2,1,0:T(8,128)(2,1)} custom-call(bf16[2,6,16,256]{3,2,1,0:T(8,128)(2,1)} %sum.1.rows), custom_call_target="tpu_custom_call" | custom-call | tf_op jit(solution)/shard_map/deliver/pallas_call | solution.py:57
  129.3 0.6 broadcast_in_dim.17.keep
  129.9 3.8 %moments.1 = (f32[2,256,256]{2,1,0:T(8,128)}, f32[2,256,256]{2,1,0:T(8,128)}, f32[8,128]{1,0:T(8,128)}) custom-call(bf16[16,6,16,256]{3,2,1,0:T(8,128)(2,1)} %deliver.1.stats, f32[1,256,512]{2,1,0:T(8,128)} %k_factor.3, f32[1,256,512]{2,1,0:T(8,128)} %c_factor.3, f32[8,128]{1,0:T(8,128)} %broadcast_in_dim.17.keep), custom_call_target="tpu_custom_call" | custom-call | tf_op jit(solution)/shard_map/moments/pallas_call | solution.py:57
  133.7 52.7 %traces.1 = (f32[32,8,128]{2,1,0:T(8,128)}, bf16[32,48,256]{2,1,0:T(8,128)(2,1)}) custom-call(f32[8,128]{1,0:T(8,128)} %get-tuple-element.28.refs_0_, bf16[48,256]{1,0:T(8,128)(2,1)} %get-tuple-element.29.refs_1_), custom_call_target="tpu_custom_call" | custom-call | tf_op jit(solution)/shard_map/traces/pallas_call | solution.py:57
  187.0 0.6 broadcast_in_dim.18.total
  187.6 7.5 %advance.1 = (f32[1,256,512]{2,1,0:T(8,128)}, f32[1,256,512]{2,1,0:T(8,128)}, f32[1,256,512]{2,1,0:T(8,128)}, f32[1,256,512]{2,1,0:T(8,128)}, bf16[512,256]{1,0:...) custom-call(f32[32,8,128]{2,1,0:T(8,128)} %get-tuple-element.30.tr, f32[8,128]{1,0:T(8,128)} %broadcast_in_dim.18.total, ...), custom_call_target="tpu_custom_call" | custom-call | tf_op jit(solution)/shard_map/advance/pallas_call | solution.py:57
  195.1 22.5 %border.1 = (bf16[32,32,256]{2,1,0:T(8,128)(2,1)}, bf16[4,16,256]{2,1,0:T(8,128)(2,1)}) custom-call(bf16[32,32,256]{2,1,0:T(8,128)(2,1)} %get-tuple-element.39.lead, bf16[512,256]{1,0:T(8,128)(2,1)} %get-tuple-element.40.c_half), custom_call_target="tpu_custom_call" | custom-call | tf_op jit(solution)/shard_map/border/pallas_call | solution.py:57
  217.7 1.7 border_sum.1.lead
  219.4 32.5 %factors.1 = (bf16[32,4,16,256]{3,2,1,0:T(8,128)(2,1)}, bf16[32,32,256]{2,1,0:T(8,128)(2,1)}) custom-call(bf16[4,16,256]{2,1,0:T(8,128)(2,1)} %get-tuple-element.41.c_part, bf16[32,256]{1,0:T(8,128)(2,1)} %border_sum.1.lead), custom_call_target="tpu_custom_call" | custom-call | tf_op jit(solution)/shard_map/factors/pallas_call | solution.py:57
  251.9 0.6 broadcast_in_dim.20.first_flag
  252.5 2.4 second.1
  254.9 11.6 %rows.1.lead_rows = bf16[256,256]{1,0:T(8,128)(2,1)} custom-call(bf16[1024,256]{1,0:T(8,128)(2,1)} %second.1), custom_call_target="tpu_custom_call" | custom-call | tf_op jit(solution)/shard_map/rows/pallas_call | solution.py:57
  266.6 3.6 %third.1 = (f32[1024,256]{1,0:T(8,128)}, bf16[256,256]{1,0:T(8,128)(2,1)}) custom-call(bf16[1024,256]{1,0:T(8,128)(2,1)} %second.1, bf16[256,256]{1,0:T(8,128)(2,1)} %rows.1.lead_rows, bf16[32,4,16,256]{3,2,1,0:T(8,128)(2,1)} %get-tuple-element.44.pieces), custom_call_target="tpu_custom_call" | custom-call | tf_op jit(solution)/shard_map/third/pallas_call | solution.py:57
  270.2 10.2 %terms.1 = bf16[8,256,256]{2,1,0:T(8,128)(2,1)} custom-call(bf16[256,256]{1,0:T(8,128)(2,1)} %get-tuple-element.46.term), custom_call_target="tpu_custom_call" | custom-call | tf_op jit(solution)/shard_map/terms/pallas_call | solution.py:57
  280.4 0.6 broadcast_in_dim.19.flag
  281.0 2.6 final.1

commit v2 on v0

v2 whole, which is shorter than its diff:
```python
import functools

import jax
import jax.numpy as jnp
from jax import lax
from jax.experimental import pallas as pl
from jax.experimental.pallas import tpu as pltpu
from jax.sharding import PartitionSpec as P

MESH = pl.DeviceIdType.MESH
highest = lax.Precision.HIGHEST
f32 = jnp.float32
bf16 = jnp.bfloat16

damping = 0.1
momentum_rate = 0.5
step_rate = 0.2

NX, NY, NZ = 4, 4, 8


def position():
    d = lax.axis_index("dp")
    f = lax.axis_index("fsdp")
    return lax.div(f, NZ), lax.div(d, 2), lax.rem(f, NZ), lax.rem(d, 2)


def device(x, y, z, c):
    return (y * 2 + c, x * NZ + z)


def class_of(x, y, z, c):
    return lax.rem(x, 2) * 8 + lax.rem(y, 2) * 4 + c * 2 + lax.rem(z, 2)


def send(src, dst, send_sem, recv_sem, target):
    return pltpu.make_async_remote_copy(
        src_ref=src, dst_ref=dst, send_sem=send_sem, recv_sem=recv_sem, device_id=target, device_id_type=MESH
    )


def arrived(dst, sem):
    pltpu.make_async_copy(dst, dst, sem).wait()


def greet(barrier, target):
    pl.semaphore_signal(barrier, inc=1, device_id=target, device_id_type=MESH)


ANY = pl.BlockSpec(memory_space=pl.ANY)
VM = pl.BlockSpec(memory_space=pltpu.VMEM)
DMA = pltpu.SemaphoreType.DMA


def call(body, name, ins, in_specs, outs, out_specs, scratch=(), cid=None):
    params = dict(collective_id=cid, has_side_effects=True) if cid is not None else {}
    return pl.pallas_call(
        body,
        out_shape=[jax.ShapeDtypeStruct(s, t) for s, t in outs],
        in_specs=in_specs,
        out_specs=out_specs,
        scratch_shapes=list(scratch),
        compiler_params=pltpu.CompilerParams(**params),
        name=name,
    )(*ins)


def token_body(
    counts, acts, grads, k_factor, c_factor, grad, xc, x0, piece_b, piece_g,
    xs, ls, b0, s1, r1, s2, r2, s3, r3, l1, s4, s5, r4,
):
    x, y, z, c = position()
    d, f = lax.axis_index("dp"), lax.axis_index("fsdp")
    barrier = pltpu.get_barrier_semaphore()

    def at(sign, a, b, g, e):
        return (
            lax.rem(x + sign * a + NX, NX),
            lax.rem(y + sign * b + NY, NY),
            lax.rem(z + sign * g + NZ, NZ),
            lax.rem(c + e, 2),
        )

    offsets = [(a, b, g, e) for a in (0, 1) for b in (0, 1) for g in (0, 1) for e in (0, 1)]
    for sign in (1, -1):
        for o in offsets:
            if o[:3] == (0, 0, 0) and (o[3] == 0 or sign == -1):
                continue
            greet(barrier, device(*at(sign, *o)))

    @pl.when(f > 0)
    def _():
        greet(barrier, (d, 0))

    limit = counts[0] * jnp.where(d == 0, 1, 0)
    for i in range(1, 8):
        limit = limit + counts[i] * jnp.where(d == i, 1, 0)
    for h in range(2):
        rows = slice(h * 64, h * 64 + 64)
        slots = lax.broadcasted_iota(jnp.int32, (64, 256), 0) + (f * 128 + h * 64)
        kept = jnp.where(slots < limit, 1.0, 0.0).astype(bf16)
        for side, ref in enumerate((acts, grads)):
            lead = ref[rows, 0:256] * kept
            ls[0, h, side, :, :] = lead[:, 0:128]
            ls[1, h, side, :, :] = lead[:, 128:256]
            for k in range(16):
                for m in range(2):
                    n = m * 16 + k
                    xs[k, h, side, :, m * 256 : m * 256 + 256] = ref[rows, n * 256 : n * 256 + 256] * kept

    @pl.when(f == 0)
    def _():
        b0[0:256, :] = k_factor[0, :, 0:256].astype(bf16)
        b0[256:512, :] = c_factor[0, :, 0:256].astype(bf16)

    pl.semaphore_wait(barrier, 29 + jnp.where(f == 0, 31, 0))
    half = pl.ds(pl.multiple_of(c * 128, 128), 128)
    other_half = pl.ds(pl.multiple_of(128 - c * 128, 128), 128)
    partner = device(x, y, z, 1 - c)
    copies, leads = [], []
    for i in (14, 15, 12, 13, 10, 11, 6, 7, 8, 9, 4, 5, 2, 3, 1, 0):
        for h, sign in ((0, 1), (1, -1)):
            o = offsets[i]
            there = at(sign, *o)
            k = class_of(*there)
            slot = h * 16 + i
            if i == 0:
                one = pltpu.make_async_copy(xs.at[k, h], xc.at[:, slot], l1.at[h])
                two = pltpu.make_async_copy(ls.at[c, h], x0.at[:, slot, :, half], r2.at[slot])
            else:
                tc = there[3]
                to_half = pl.ds(pl.multiple_of(tc * 128, 128), 128)
                one = send(xs.at[k, h], xc.at[:, slot], s1.at[slot], r1.at[slot], device(*there))
                two = send(ls.at[tc, h], x0.at[:, slot, :, to_half], s2.at[slot], r2.at[slot], device(*there))
            two.start()
            one.start()
            copies.append(one)
            leads.append((i, slot, two))

    def grad_piece(t):
        return grad.at[pl.ds(pl.multiple_of(t * 32, 32), 32)]

    def lead_piece(t):
        return b0.at[pl.ds(pl.multiple_of(t * 16, 16), 16)]

    @pl.when(f == 0)
    def _():
        pltpu.make_async_copy(grad_piece(0), piece_g, r3.at[0]).start()
        pltpu.make_async_copy(lead_piece(0), piece_b, r3.at[1]).start()

        @pl.loop(1, 32)
        def _(t):
            send(grad_piece(t), piece_g, s3.at[t], r3.at[0], (d, t)).start()
            send(lead_piece(t), piece_b, s4.at[t], r3.at[1], (d, t)).start()

    passed = []
    for i, slot, two in leads:
        mine = x0.at[:, slot, :, half]
        arrived(mine, r2.at[slot])
        on = send(mine, x0.at[:, slot ^ 1, :, half], s5.at[slot], r4.at[slot ^ 1], partner)
        on.start()
        passed.append(on)
    for i, slot, two in leads:
        if i > 0:
            two.wait_send()
    for slot, on in zip([slot for _, slot, _ in leads], passed):
        on.wait_send()
        arrived(x0.at[:, slot, :, other_half], r4.at[slot])
    for one in copies:
        one.wait()
    arrived(piece_g, r3.at[0])
    arrived(piece_b, r3.at[1])

    @pl.when(f == 0)
    def _():
        @pl.loop(1, 32)
        def _(t):
            send(grad_piece(t), piece_g, s3.at[t], r3.at[0], (d, t)).wait_send()
            send(lead_piece(t), piece_b, s4.at[t], r3.at[1], (d, t)).wait_send()


def dot(a, b):
    return jnp.dot(a, b, precision=highest, preferred_element_type=f32)


def dot16(a, b):
    return jnp.dot(a, b, preferred_element_type=f32)


def stats_body(
    xc, x0, k_factor, c_factor, piece_b, piece_g, h_out, u_out, gram_out, tr_out, b0_out, g0_out,
    ps, pi, sm, st, tr, lead_b, lead_g,
    rs_s, rs_r, de_s, de_r, ag_s, zb_s, zb_r, zg_s, zg_r, xb_s, xb_r, xg_s, xg_r, tr_s, tr_r,
):
    x, y, z, c = position()
    d, f = lax.axis_index("dp"), lax.axis_index("fsdp")
    barrier = pltpu.get_barrier_semaphore()
    mine = class_of(x, y, z, c)
    xi, yi, zi = lax.div(x, 2), lax.div(y, 2), lax.div(z, 2)
    slot = xi * 8 + yi * 4 + zi
    mates = [(a, b, g) for a in range(2) for b in range(2) for g in range(4)]

    def mate(a, b, g):
        return lax.rem(x + 2 * a, NX), lax.rem(y + 2 * b, NY), lax.rem(z + 2 * g, NZ)

    to_d = lax.rem(y + lax.rem(zi, 2), NY) * 2 + lax.div(zi, 2)
    k = lax.rem(f, 16)
    px, py, pc, pz = lax.div(k, 8), lax.rem(lax.div(k, 4), 2), lax.rem(lax.div(k, 2), 2), lax.rem(k, 2)
    shift = lax.rem(y + py, 2)
    from_y = lax.rem(y - shift + NY, NY)
    from_zi = 2 * c + shift
    from_j = [i * 8 + lax.div(from_y, 2) * 4 + from_zi for i in range(2)]
    from_at = [device(px + 2 * i, from_y, pz + 2 * from_zi, pc) for i in range(2)]

    def is_me(there):
        return jnp.logical_and(there[0] == d, there[1] == f)

    for o in mates[1:]:
        greet(barrier, device(*mate(*o), c))

    @pl.loop(1, 32)
    def _(t):
        greet(barrier, (d, lax.rem(f + t, 32)))

    for t in range(1, 8):
        greet(barrier, (lax.rem(d + t, 8), f))
    for there in from_at:

        @pl.when(jnp.logical_not(is_me(there)))
        def _():
            greet(barrier, there)

    dims = (((0,), (0,)), ((), ()))

    def gram(side):
        lead = x0[side]
        a = xc[side, :, 0:256]
        b = xc[side, :, 256:512]
        for i, (left, right) in enumerate(((a, a), (b, b), (lead, a), (lead, b), (lead, lead))):
            g = lax.dot_general(left, right, dims, preferred_element_type=f32)
            ps[side, :, i, :, :] = g.astype(bf16).reshape(16, 16, 256)

    def scatter(side):
        copies = []
        for i, o in enumerate(mates):
            if i > 0:
                tx, ty, tz = mate(*o)
                j = lax.div(tx, 2) * 8 + lax.div(ty, 2) * 4 + lax.div(tz, 2)
                copy = send(ps.at[side, j], pi.at[side, i], rs_s.at[side, i], rs_r.at[side, i], device(tx, ty, tz, c))
                copy.start()
                copies.append(copy)
        return copies

    gram(0)
    to_self = jnp.where(is_me((to_d, mine)), 1, 0) + jnp.where(is_me((to_d, mine + 16)), 1, 0)
    pl.semaphore_wait(barrier, 15 + 31 + 7 + 2 - to_self)
    first = scatter(0)
    own_b = pltpu.make_async_copy(piece_b, lead_b.at[x, z], zb_r.at[0])
    own_g = pltpu.make_async_copy(piece_g, lead_g.at[x, z], zg_r.at[0])
    own_b.start()
    own_g.start()
    for t in range(1, 8):
        there = (d, x * NZ + lax.rem(z + t, NZ))
        send(piece_b, lead_b.at[x, z], zb_s.at[t], zb_r.at[t], there).start()
        send(piece_g, lead_g.at[x, z], zg_s.at[t], zg_r.at[t], there).start()
    gram(1)
    second = scatter(1)

    flag = jnp.where(f > 0, 1.0, 0.0)
    factors = []
    for side, factor in enumerate((k_factor, c_factor)):
        diag = factor[0, :, 0:256]
        border = factor[0, :, 256:512] * flag
        gram_out[side] = dot(diag.T, diag) + dot(border.T, border)
        factors.append((diag, border))

    def total(side, copies):
        for copy in copies:
            copy.wait()
        value = ps[side, slot].astype(f32)
        for i in range(1, 16):
            value = value + pi[side, i].astype(f32)
        value = value.astype(bf16)
        for m in range(2):
            for q, source in enumerate((m, 2 + m, 4)):
                sm[side, m, q] = value[source]

    def deliver(side):
        for m in range(2):
            there = (to_d, mine + 16 * m)

            @pl.when(is_me(there))
            def _():
                pltpu.make_async_copy(sm.at[side, m], st.at[side, slot], de_r.at[side, slot]).start()

            @pl.when(jnp.logical_not(is_me(there)))
            def _():
                send(sm.at[side, m], st.at[side, slot], de_s.at[side, m], de_r.at[side, slot], there).start()

    def share(side):
        for i in range(2):
            j = from_j[i]
            arrived(st.at[side, j], de_r.at[side, j])
            for t in range(1, 8):
                there = (lax.rem(d + t, 8), f)
                send(st.at[side, j], st.at[side, j], ag_s.at[side, i, t], de_r.at[side, j], there).start()

    total(0, first)
    deliver(0)
    own_b.wait()
    own_g.wait()
    for t in range(1, 8):
        there = (d, x * NZ + lax.rem(z + t, NZ))
        behind = lax.rem(z + NZ - t, NZ)
        send(piece_b, lead_b.at[x, z], zb_s.at[t], zb_r.at[t], there).wait_send()
        send(piece_g, lead_g.at[x, z], zg_s.at[t], zg_r.at[t], there).wait_send()
        arrived(lead_b.at[x, behind], zb_r.at[t])
        arrived(lead_g.at[x, behind], zg_r.at[t])
    total(1, second)
    deliver(1)
    share(0)
    share(1)
    for t in range(1, 4):
        there = (d, lax.rem(x + t, NX) * NZ + z)
        send(lead_b.at[x], lead_b.at[x], xb_s.at[t], xb_r.at[t], there).start()
        send(lead_g.at[x], lead_g.at[x], xg_s.at[t], xg_r.at[t], there).start()

    rows = lax.broadcasted_iota(jnp.int32, (256, 256), 0)
    cols = lax.broadcasted_iota(jnp.int32, (256, 256), 1)
    for side, (diag, border) in enumerate(factors):
        for j in range(16):
            mine_too = jnp.logical_or(from_j[0] == j, from_j[1] == j)

            @pl.when(jnp.logical_not(mine_too))
            def _():
                arrived(st.at[side, j], de_r.at[side, j])

        a = st[side, :, 0].reshape(256, 256)
        cross = st[side, :, 1].reshape(256, 256)
        lead = st[side, :, 2].reshape(256, 256)
        diag16, border16 = diag.astype(bf16), border.astype(bf16)
        u = dot16(cross, diag16) + dot16(lead, border16)
        v = dot16(a, diag16) + dot16(cross.T, border16)
        h = dot(diag16.astype(f32).T, v) + dot(border16.astype(f32).T, u)
        u_out[side] = u
        h_out[side] = h
        tr_h = jnp.sum(jnp.where(rows == cols, h, 0.0))
        tr_g = jnp.sum(diag * diag) + jnp.sum(border * border)
        tr[f, side * 2 : side * 2 + 1, :] = jnp.full((1, 128), tr_h, f32)
        tr[f, side * 2 + 1 : side * 2 + 2, :] = jnp.full((1, 128), tr_g, f32)
    tr[f, 4:8, :] = jnp.zeros((4, 128), f32)

    @pl.loop(1, 32)
    def _(t):
        send(tr.at[f], tr.at[f], tr_s.at[t], tr_r.at[t], (d, lax.rem(f + t, 32))).start()

    for t in range(1, 4):
        there = (d, lax.rem(x + t, NX) * NZ + z)
        behind = lax.rem(x + NX - t, NX)
        send(lead_b.at[x], lead_b.at[x], xb_s.at[t], xb_r.at[t], there).wait_send()
        send(lead_g.at[x], lead_g.at[x], xg_s.at[t], xg_r.at[t], there).wait_send()
        arrived(lead_b.at[behind], xb_r.at[t])
        arrived(lead_g.at[behind], xg_r.at[t])
    b0_out[...] = lead_b[...].reshape(512, 256)
    g0_out[...] = lead_g[...].reshape(1024, 256)
    for side in range(2):
        for m in range(2):
            there = (to_d, mine + 16 * m)

            @pl.when(jnp.logical_not(is_me(there)))
            def _():
                send(sm.at[side, m], st.at[side, slot], de_s.at[side, m], de_r.at[side, slot], there).wait_send()

        for i in range(2):
            j = from_j[i]
            for t in range(1, 8):
                there = (lax.rem(d + t, 8), f)
                send(st.at[side, j], st.at[side, j], ag_s.at[side, i, t], de_r.at[side, j], there).wait_send()

    @pl.loop(1, 32)
    def _(t):
        send(tr.at[f], tr.at[f], tr_s.at[t], tr_r.at[t], (d, lax.rem(f + t, 32))).wait_send()
        arrived(tr.at[lax.rem(f + 32 - t, 32)], tr_r.at[t])

    sums = tr[0]
    for i in range(1, 32):
        sums = sums + tr[i]
    tr_out[...] = sums


def advance_body(
    counts, traces, h_in, u_in, gram_in, k_factor, c_factor, k_moment, c_moment, leads,
    k_new, c_new, km_new, cm_new, k_half, c_half,
):
    f = lax.axis_index("fsdp")
    flag = jnp.where(f > 0, 1.0, 0.0)
    tokens = counts[0]
    for i in range(1, 8):
        tokens = tokens + counts[i]
    inverse = 1.0 / jnp.full((1, 1), tokens.astype(f32), f32)
    width = 8192.0
    trace = [traces[i : i + 1, 0:1] for i in range(4)]
    rows = lax.broadcasted_iota(jnp.int32, (256, 256), 0)
    cols = lax.broadcasted_iota(jnp.int32, (256, 256), 1)
    identity = jnp.where(rows == cols, 1.0, 0.0)
    for side, (factor, moment, f_new, m_new, half) in enumerate(
        ((k_factor, k_moment, k_new, km_new, k_half), (c_factor, c_moment, c_new, cm_new, c_half))
    ):
        other_h = trace[2 - 2 * side] * inverse * inverse
        other_g = trace[3 - 2 * side] * damping
        diag = factor[0, :, 0:256]
        border = factor[0, :, 256:512] * flag
        lead = leads[side * 256 : side * 256 + 256, :].astype(f32)
        fresh = (other_h * h_in[side] + other_g * gram_in[side] - width * identity) / (2.0 * width)
        cross = dot(lead.T, other_h * u_in[side] + other_g * border) * flag / (2.0 * width)
        m_diag = momentum_rate * moment[0, :, 0:256] + fresh
        m_side = (momentum_rate * moment[0, :, 256:512] + cross) * flag
        n_diag = diag - step_rate * dot(diag, m_diag)
        n_side = (border - step_rate * (dot(lead, m_side) + dot(border, m_diag))) * flag
        f_new[0, :, 0:256] = n_diag
        f_new[0, :, 256:512] = n_side
        m_new[0, :, 0:256] = m_diag
        m_new[0, :, 256:512] = m_side
        half[0:256, :] = n_diag.astype(bf16)
        half[256:512, :] = n_side.astype(bf16)


def precond_body(
    k_half, c_half, grad, grad_lead, out,
    lead_src, lead_in, own, lead_sum, all_lead, second, lead_rows, cb, term, terms, part,
    rs_s, rs_r, ga_s, ga_r, ca_s, ca_r, cz_s, cz_r, cx_s, cx_r, ro_s, ro_r, te_s, te_r,
):
    x, y, z, c = position()
    d, f = lax.axis_index("dp"), lax.axis_index("fsdp")
    barrier = pltpu.get_barrier_semaphore()

    @pl.loop(1, 32)
    def _(t):
        greet(barrier, (d, lax.rem(f + t, 32)))

    @pl.when(d == 0)
    def _():
        for t in range(1, 8):
            greet(barrier, (t, f))

    @pl.when(d > 0)
    def _():
        greet(barrier, (0, f))

    k_diag, k_side = k_half[0:256, :], k_half[256:512, :]
    first = (dot16(grad[...], k_diag) + dot16(grad_lead[...], k_side)).astype(bf16)
    lead_src[...] = dot16(first, k_side.T).astype(bf16).reshape(32, 32, 256)
    pl.semaphore_wait(barrier, 31 + jnp.where(d == 0, 7, 1))

    holder = lax.div(z, 4) == c
    root = jnp.logical_and(holder, x == y)
    j = lax.rem(z, 4)

    def quarter(t):
        return c_half.at[pl.ds(pl.multiple_of(t * 128, 128), 128)]

    def scatter_copy(t):
        to = lax.rem(x + t, NX)
        return send(quarter(to), cb.at[to, j], ca_s.at[t], ca_r, (d, to * NZ + z))

    @pl.when(root)
    def _():
        for t in range(1, 4):
            scatter_copy(t).start()
        pltpu.make_async_copy(quarter(x), cb.at[x, j], ca_r).start()

    own_piece = pltpu.make_async_copy(lead_src.at[f], lead_in.at[f], rs_r.at[0])
    own_piece.start()

    @pl.loop(1, 32)
    def _(t):
        there = lax.rem(f + t, 32)
        send(lead_src.at[there], lead_in.at[f], rs_s.at[t], rs_r.at[t], (d, there)).start()

    own[...] = dot16(first, k_diag.T)

    def ring_copy(t):
        return send(cb.at[x, j], cb.at[x, j], cz_s.at[t], cz_r.at[j], (d, x * NZ + lax.rem(z + t, NZ)))

    @pl.when(holder)
    def _():
        arrived(cb.at[x, j], ca_r)
        for t in range(1, 8):
            ring_copy(t).start()

    own_piece.wait()

    @pl.loop(1, 32)
    def _(t):
        there = lax.rem(f + t, 32)
        send(lead_src.at[there], lead_in.at[f], rs_s.at[t], rs_r.at[t], (d, there)).wait_send()
        arrived(lead_in.at[lax.rem(f + 32 - t, 32)], rs_r.at[t])

    total = lead_in[0].astype(f32)
    for i in range(1, 32):
        total = total + lead_in[i].astype(f32)
    lead_sum[...] = total.astype(bf16)
    second[...] = own[...].astype(bf16)

    @pl.when(f > 0)
    def _():
        send(lead_sum, all_lead.at[f], ga_s, ga_r.at[f], (d, 0)).start()

    for i in range(4):

        @pl.when(jnp.logical_or(jnp.logical_not(holder), j != i))
        def _():
            arrived(cb.at[x, i], cz_r.at[i])

    def spread_copy(t):
        return send(cb.at[x], cb.at[x], cx_s.at[t], cx_r.at[t], (d, lax.rem(x + t, NX) * NZ + z))

    for t in range(1, 4):
        spread_copy(t).start()

    @pl.when(f == 0)
    def _():
        all_lead[0] = lead_sum[...]
        for i in range(1, 32):
            arrived(all_lead.at[i], ga_r.at[i])
        second[...] = (own[...] + all_lead[...].reshape(1024, 256).astype(f32)).astype(bf16)

    src = second.at[0:256]

    @pl.when(d == 0)
    def _():
        for t in range(1, 8):
            send(src, lead_rows, ro_s.at[t], ro_r, (t, f)).start()
        pltpu.make_async_copy(src, lead_rows, ro_r).start()

    for t in range(1, 4):
        arrived(cb.at[lax.rem(x + NX - t, NX)], cx_r.at[t])
    for i in range(4):
        diag = cb[0:2, i].reshape(256, 256)
        part[i] = dot16(diag.T, second[i * 256 : i * 256 + 256, :])
    arrived(lead_rows, ro_r)
    sum_term = jnp.zeros((256, 256), f32)
    for i in range(4):
        diag = cb[0:2, i].reshape(256, 256)
        side = cb[2:4, i].reshape(256, 256)
        third = (part[i] + dot16(side.T, lead_rows[...])).astype(bf16)
        own[i * 256 : i * 256 + 256, :] = dot16(diag, third)
        sum_term = sum_term + dot16(side, third)
    term[...] = sum_term.astype(bf16)

    @pl.when(d > 0)
    def _():
        send(term, terms.at[d], te_s, te_r.at[d], (0, f)).start()

    out[256:1024, :] = own[256:1024, :].astype(bf16)

    @pl.when(d > 0)
    def _():
        out[0:256, :] = own[0:256, :].astype(bf16)
        send(term, terms.at[d], te_s, te_r.at[d], (0, f)).wait_send()

    @pl.when(d == 0)
    def _():
        whole = own[0:256, :] + sum_term
        for t in range(1, 8):
            arrived(terms.at[t], te_r.at[t])
            whole = whole + terms[t].astype(f32)
        out[0:256, :] = whole.astype(bf16)
        for t in range(1, 8):
            send(src, lead_rows, ro_s.at[t], ro_r, (t, f)).wait_send()

    @pl.when(root)
    def _():
        for t in range(1, 4):
            scatter_copy(t).wait_send()

    @pl.when(holder)
    def _():
        for t in range(1, 8):
            ring_copy(t).wait_send()

    for t in range(1, 4):
        spread_copy(t).wait_send()

    @pl.when(f > 0)
    def _():
        send(lead_sum, all_lead.at[f], ga_s, ga_r.at[f], (d, 0)).wait_send()


def per_device(acts, out_grads, token_counts, k_factor, c_factor, k_moment, c_moment, grad_weight):
    SM = pl.BlockSpec(memory_space=pltpu.SMEM)
    V = pltpu.VMEM
    xc, x0, piece_b, piece_g = call(
        token_body, "tokens", (token_counts, acts, out_grads, k_factor, c_factor, grad_weight), [SM] + [VM] * 5,
        [((2, 32, 64, 512), bf16), ((2, 32, 64, 256), bf16), ((16, 256), bf16), ((32, 256), bf16)], [ANY] * 4,
        [V((16, 2, 2, 64, 512), bf16), V((2, 2, 2, 64, 128), bf16), V((512, 256), bf16)]
        + [DMA((32,))] * 5 + [DMA((2,)), DMA((2,)), DMA((32,)), DMA((32,)), DMA((32,))],
        0,
    )
    h, u, grams, traces, leads, grad_lead = call(
        stats_body, "stats",
        (xc.reshape(2, 2048, 512), x0.reshape(2, 2048, 256), k_factor, c_factor, piece_b, piece_g),
        [VM] * 4 + [ANY] * 2,
        [((2, 256, 256), f32)] * 3 + [((8, 128), f32), ((512, 256), bf16), ((1024, 256), bf16)], [VM] * 6,
        [V((2, 16, 5, 16, 256), bf16), V((2, 16, 5, 16, 256), bf16), V((2, 2, 3, 16, 256), bf16),
         V((2, 16, 3, 16, 256), bf16), V((32, 8, 128), f32), V((4, 8, 16, 256), bf16), V((4, 8, 32, 256), bf16),
         DMA((2, 16)), DMA((2, 16)), DMA((2, 2)), DMA((2, 16)), DMA((2, 2, 8)), DMA((8,)), DMA((8,)), DMA((8,)),
         DMA((8,)), DMA((4,)), DMA((4,)), DMA((4,)), DMA((4,)), DMA((32,)), DMA((32,))],
        1,
    )
    k_new, c_new, km_new, cm_new, k_half, c_half = call(
        advance_body, "advance",
        (token_counts, traces, h, u, grams, k_factor, c_factor, k_moment, c_moment, leads), [SM] + [VM] * 9,
        [((1, 256, 512), f32)] * 4 + [((512, 256), bf16)] * 2, [VM] * 6,
    )
    (precond,) = call(
        precond_body, "precond", (k_half, c_half, grad_weight, grad_lead), [VM] * 4, [((1024, 256), bf16)], [VM],
        [V((32, 32, 256), bf16), V((32, 32, 256), bf16), V((1024, 256), f32), V((32, 256), bf16),
         V((32, 32, 256), bf16), V((1024, 256), bf16), V((256, 256), bf16), V((4, 4, 128, 256), bf16),
         V((256, 256), bf16), V((8, 256, 256), bf16), V((4, 256, 256), f32),
         DMA((32,)), DMA((32,)), DMA, DMA((32,)), DMA((4,)), DMA, DMA((8,)), DMA((4,)), DMA((4,)), DMA((4,)),
         DMA((8,)), DMA, DMA, DMA((8,))],
        2,
    )
    return k_new, c_new, km_new, cm_new, precond


def solution(mesh):
    in_specs = (
        P(("dp", "fsdp"), None),
        P(("dp", "fsdp"), None),
        P(),
        P("fsdp", None, None),
        P("fsdp", None, None),
        P("fsdp", None, None),
        P("fsdp", None, None),
        P("dp", "fsdp"),
    )
    out_specs = (
        P("fsdp", None, None),
        P("fsdp", None, None),
        P("fsdp", None, None),
        P("fsdp", None, None),
        P("dp", "fsdp"),
    )
    return jax.shard_map(per_device, mesh=mesh, in_specs=in_specs, out_specs=out_specs, check_vma=False)
```

time: 1120 us -> 185 us (0.17)
  waiting for transfers between devices: 867 us -> 0 us
  Pallas kernels: 0 us -> 182 us
  blocking collectives: 136 us -> 0 us
  matrix products: 34.6 us -> 0 us
  local copies, waits for them, and re-layouts: 31.9 us -> 1.87 us
  other arithmetic: 25.8 us -> 0 us
  between operations: 20.5 us -> 0.66 us
    psum x8 -> x0, waiting for transfers between devices: 822 us -> none  [the longest x5 639 us: spread(): return lax.psum(kept, axis)]
    pallas_call x0 -> x4, Pallas kernels: none -> 182 us  [call(): pl.pallas_call(body, out_shape=[jax.ShapeDtypeStruct(s, t) for s, t in ou...]
    psum x1 -> x0, blocking collectives: 75.2 us -> none  [per_device(): totals = lax.psum(local_traces, 'fsdp')]
    all_to_all x1 -> x0, blocking collectives: 60.6 us -> none  [to_owners(): lax.all_to_all(pair[0], 'fsdp', split_axis=1, concat_axis=0, tiled=True)]
    all_to_all x1 -> x0, waiting for transfers between devices: 45.5 us -> none  [to_owners(): lax.all_to_all(pair[1], 'fsdp', split_axis=1, concat_axis=0, tiled=True)]
    dot_general x28 -> x0, matrix products: 34.6 us -> none  [the longest x2 8.14 us: block_stats(): jnp.einsum('ti,tnj->nij', lead_image, blocked, preferred_element_type=jnp...]
    unnamed x55 -> x1, local copies, waits for them, and re-layouts: 16.3 us -> 1.87 us
  transfers between devices with their start and end apart: 9 -> 0, of which waited for: 9 -> 0; matrix products, arithmetic and copies ran while one was open for 3% -> 0% of each run, Pallas kernels for 0% -> 0%
where the time goes in v2:
time: 185 us
  Pallas kernels  182 us (98%)
  local copies, waits for them, and re-layouts  1.87 us (1%)
    pallas_call x4, Pallas kernels, call(): pl.pallas_call(body, out_shape=[jax.ShapeDtypeStruct(s, t) for s, t in ou...  182 us

profile of v2, /device:TPU:0, one launch (start us, length us, event | category | flops | bytes accessed | tf_op | source)
XLA Modules:
  0.0 184.6 jit_solution(17996060369824673035)
XLA Ops:
  0.6 52.9 %tokens.1 = (bf16[2,32,64,512]{3,2,1,0:T(8,128)(2,1)}, bf16[2,32,64,256]{3,2,1,0:T(8,128)(2,1)}, bf16[16,256]{1,0:T(8,128)(2,1)}, bf16[32,256]{1,0:T(8,128)(2,1)}) custom-call(s32[8]{0:T(128)} %counts.3, bf16[128,8192]{1,0:T(8,128)(2,1)} %acts.1, bf16[128,8192]{1,0:T(8,128)(2,1)} %grads.1, f32[1,256,512]{2,1,0:T(8,128)} %k_factor.5, ...), custom_call_target="tpu_custom_call" | custom-call | tf_op jit(solution)/shard_map/tokens/pallas_call | solution.py:57
  53.5 72.7 %stats.1 = (f32[2,256,256]{2,1,0:T(8,128)}, f32[2,256,256]{2,1,0:T(8,128)}, f32[2,256,256]{2,1,0:T(8,128)}, f32[8,128]{1,0:T(8,128)}, bf16[512,256]{1,0:T(8,128)(2,1)}, /*index=5*/bf16[1024,256]{1,0:T(8,128)(2,1)}) custom-call(bf16[2,2048,512]{2,1,0:T(8,128)(2,1)} %bitcast.2, bf16[2,2048,256]{2,1,0:T(8,128)(2,1)} %bitcast.3, f32[1,256,512]{2,1,0:T(8,128)} %k_factor.5, ...), custom_call_target="tpu_custom_call" | custom-call | tf_op jit(solution)/shard_map/stats/pallas_call | solution.py:57
  126.2 5.4 %advance.1 = (f32[1,256,512]{2,1,0:T(8,128)}, f32[1,256,512]{2,1,0:T(8,128)}, f32[1,256,512]{2,1,0:T(8,128)}, f32[1,256,512]{2,1,0:T(8,128)}, bf16[512,256]{1,0:T(8,128)(2,1)}, /*index=5*/bf16[512,256]{1,0:T(8,128)(2,1)}) custom-call(s32[8]{0:T(128)} %counts.3, f32[8,128]{1,0:T(8,128)} %get-tuple-element.25.traces, f32[2,256,256]{2,1,0:T(8,128)} %get-tuple-element.26.h_in, ...), custom_call_target="tpu_custom_call" | custom-call | tf_op jit(solution)/shard_map/advance/pallas_call | solution.py:57
  131.6 51.1 %precond.1 = bf16[1024,256]{1,0:T(8,128)(2,1)} custom-call(bf16[512,256]{1,0:T(8,128)(2,1)} %get-tuple-element.34.k_half, bf16[512,256]{1,0:T(8,128)(2,1)} %get-tuple-element.35.c_half, bf16[1024,256]{1,0:T(8,128)(2,1)} %grad.3, bf16[1024,256]{1,0:T(8,128)(2,1)} %get-tuple-element.36.grad_lead), custom_call_target="tpu_custom_call" | custom-call | tf_op jit(solution)/shard_map/precond/pallas_call | solution.py:57
  182.8 1.9 %copy.14 = bf16[1024,256]{1,0:T(8,128)(2,1)} copy(bf16[1024,256]{1,0:T(8,128)(2,1)} %precond.1) | data formatting | bytes 1048576

commit v3 on v2

--- a/solution.py
+++ b/solution.py
@@ -65,15 +65,29 @@
     )(*ins)
 
 
-def token_body(
-    counts, acts, grads, k_factor, c_factor, grad, xc, x0, piece_b, piece_g,
-    xs, ls, b0, s1, r1, s2, r2, s3, r3, l1, s4, s5, r4,
+def dot(a, b):
+    return jnp.dot(a, b, precision=highest, preferred_element_type=f32)
+
+
+def dot16(a, b):
+    return jnp.dot(a, b, preferred_element_type=f32)
+
+
+def stats_body(
+    counts, acts, grads, k_factor, c_factor, grad, h_out, u_out, gram_out, tr_out, b0_out, g0_out,
+    raw, xs, ls, xc, x0, b0, piece_b, piece_g, ps, pi, sm, st, tr, lead_b, lead_g,
+    in_s, s1, r1, s2, r2, s5, r4, s3, s4, r3,
+    rs_s, rs_r, de_s, de_r, a0_s, a0_r, ag_s, fw_s, zb_s, zb_r, zg_s, zg_r, xb_s, xb_r, xg_s, xg_r, tr_s, tr_r,
 ):
     x, y, z, c = position()
     d, f = lax.axis_index("dp"), lax.axis_index("fsdp")
     barrier = pltpu.get_barrier_semaphore()
-
-    def at(sign, a, b, g, e):
+    loads = [pltpu.make_async_copy(ref, raw.at[i], in_s.at[i]) for i, ref in enumerate((acts, grads))]
+    for one in loads:
+        one.start()
+    partner = device(x, y, z, 1 - c)
+
+    def cell(sign, a, b, g, e):
         return (
             lax.rem(x + sign * a + NX, NX),
             lax.rem(y + sign * b + NY, NY),
@@ -82,66 +96,135 @@
         )
 
     offsets = [(a, b, g, e) for a in (0, 1) for b in (0, 1) for g in (0, 1) for e in (0, 1)]
+    mine = class_of(x, y, z, c)
+    xi, yi, zi = lax.div(x, 2), lax.div(y, 2), lax.div(z, 2)
+    slot = xi * 8 + yi * 4 + zi
+    mates = [(a, b, g) for a in range(2) for b in range(2) for g in range(4)]
+
+    def mate(a, b, g):
+        return lax.rem(x + 2 * a, NX), lax.rem(y + 2 * b, NY), lax.rem(z + 2 * g, NZ)
+
+    k = lax.rem(f, 16)
+    px, py, pc, pz = lax.div(k, 8), lax.rem(lax.div(k, 4), 2), lax.rem(lax.div(k, 2), 2), lax.rem(k, 2)
+
+    def group_for(parity):
+        return lax.rem(2 * yi + parity + lax.rem(zi, 2), NY) * 2 + lax.div(zi, 2)
+
+    def slots_at(there_y):
+        shift = lax.rem(there_y + py, 2)
+        low = lax.div(lax.rem(there_y - shift + NY, NY), 2) * 4 + 2 * c + shift
+        return [low, low + 8]
+
+    def owner(j, qx, qy, qz, qc):
+        return device(qx + 2 * lax.div(j, 8), qy + 2 * lax.rem(lax.div(j, 4), 2), qz + 2 * lax.rem(j, 4), qc)
+
+    to_d = group_for(lax.rem(y, 2))
+    from_j = slots_at(y)
+
+    def is_me(there):
+        return jnp.logical_and(there[0] == d, there[1] == f)
+
+    def lead_target(t):
+        return (group_for(lax.rem(lax.div(t, 4), 2)), t)
+
     for sign in (1, -1):
         for o in offsets:
             if o[:3] == (0, 0, 0) and (o[3] == 0 or sign == -1):
                 continue
-            greet(barrier, device(*at(sign, *o)))
-
-    @pl.when(f > 0)
-    def _():
-        greet(barrier, (d, 0))
+            greet(barrier, device(*cell(sign, *o)))
+    for o in mates[1:]:
+        greet(barrier, device(*mate(*o), c))
+
+    @pl.loop(1, 32)
+    def _(t):
+        greet(barrier, (d, lax.rem(f + t, 32)))
+
+    for t in range(1, 4):
+        greet(barrier, device(x, lax.rem(y + t, NY), z, c))
+    for j in from_j:
+        for there in (owner(j, px, py, pz, pc), owner(j, 0, 0, 0, 0)):
+
+            @pl.when(jnp.logical_not(is_me(there)))
+            def _():
+                greet(barrier, there)
 
     limit = counts[0] * jnp.where(d == 0, 1, 0)
     for i in range(1, 8):
         limit = limit + counts[i] * jnp.where(d == i, 1, 0)
+    kept = []
     for h in range(2):
-        rows = slice(h * 64, h * 64 + 64)
-        slots = lax.broadcasted_iota(jnp.int32, (64, 256), 0) + (f * 128 + h * 64)
-        kept = jnp.where(slots < limit, 1.0, 0.0).astype(bf16)
-        for side, ref in enumerate((acts, grads)):
-            lead = ref[rows, 0:256] * kept
-            ls[0, h, side, :, :] = lead[:, 0:128]
-            ls[1, h, side, :, :] = lead[:, 128:256]
-            for k in range(16):
+        at_slot = lax.broadcasted_iota(jnp.int32, (64, 256), 0) + (f * 128 + h * 64)
+        kept.append(jnp.where(at_slot < limit, 1.0, 0.0).astype(bf16))
+
+    def mask(side):
+        loads[side].wait()
+        for h in range(2):
+            rows = slice(h * 64, h * 64 + 64)
+            lead = raw[side, rows, 0:256] * kept[h]
+            ls[side, 0, h, :, :] = lead[:, 0:128]
+            ls[side, 1, h, :, :] = lead[:, 128:256]
+            for i in range(16):
                 for m in range(2):
-                    n = m * 16 + k
-                    xs[k, h, side, :, m * 256 : m * 256 + 256] = ref[rows, n * 256 : n * 256 + 256] * kept
+                    n = m * 16 + i
+                    cols = slice(m * 256, m * 256 + 256)
+                    xs[side, i, h, :, cols] = raw[side, rows, n * 256 : n * 256 + 256] * kept[h]
+
+    half = pl.ds(pl.multiple_of(c * 128, 128), 128)
+    other_half = pl.ds(pl.multiple_of(128 - c * 128, 128), 128)
+
+    def exchange(side):
+        copies = []
+        for i in (14, 15, 12, 13, 10, 11, 6, 7, 8, 9, 4, 5, 2, 3, 1, 0):
+            for h, sign in ((0, 1), (1, -1)):
+                there = cell(sign, *offsets[i])
+                to = class_of(*there)
+                at = h * 16 + i
+                if i == 0:
+                    one = pltpu.make_async_copy(xs.at[side, to, h], xc.at[side, at], r1.at[side, at])
+                    two = pltpu.make_async_copy(ls.at[side, c, h], x0.at[side, at, :, half], r2.at[side, at])
+                else:
+                    tc = there[3]
+                    to_half = pl.ds(pl.multiple_of(tc * 128, 128), 128)
+                    dst = device(*there)
+                    one = send(xs.at[side, to, h], xc.at[side, at], s1.at[side, at], r1.at[side, at], dst)
+                    two = send(ls.at[side, tc, h], x0.at[side, at, :, to_half], s2.at[side, at], r2.at[side, at], dst)
+                two.start()
+                one.start()
+                copies.append((i, at, one, two))
+        return copies
+
+    def collect(side, copies):
+        passed = []
+        for i, at, one, two in copies:
+            got = x0.at[side, at, :, half]
+            arrived(got, r2.at[side, at])
+            on = send(got, x0.at[side, at ^ 1, :, half], s5.at[side, at], r4.at[side, at ^ 1], partner)
+            on.start()
+            passed.append(on)
+        for i, at, one, two in copies:
+            arrived(xc.at[side, at], r1.at[side, at])
+        for i, at, one, two in copies:
+            arrived(x0.at[side, at, :, other_half], r4.at[side, at])
+        return passed
+
+    def grad_piece(t):
+        return grad.at[pl.ds(pl.multiple_of(t * 32, 32), 32)]
+
+    def lead_piece(t):
+        return b0.at[pl.ds(pl.multiple_of(t * 16, 16), 16)]
 
     @pl.when(f == 0)
     def _():
         b0[0:256, :] = k_factor[0, :, 0:256].astype(bf16)
         b0[256:512, :] = c_factor[0, :, 0:256].astype(bf16)
 
-    pl.semaphore_wait(barrier, 29 + jnp.where(f == 0, 31, 0))
-    half = pl.ds(pl.multiple_of(c * 128, 128), 128)
-    other_half = pl.ds(pl.multiple_of(128 - c * 128, 128), 128)
-    partner = device(x, y, z, 1 - c)
-    copies, leads = [], []
-    for i in (14, 15, 12, 13, 10, 11, 6, 7, 8, 9, 4, 5, 2, 3, 1, 0):
-        for h, sign in ((0, 1), (1, -1)):
-            o = offsets[i]
-            there = at(sign, *o)
-            k = class_of(*there)
-            slot = h * 16 + i
-            if i == 0:
-                one = pltpu.make_async_copy(xs.at[k, h], xc.at[:, slot], l1.at[h])
-                two = pltpu.make_async_copy(ls.at[c, h], x0.at[:, slot, :, half], r2.at[slot])
-            else:
-                tc = there[3]
-                to_half = pl.ds(pl.multiple_of(tc * 128, 128), 128)
-                one = send(xs.at[k, h], xc.at[:, slot], s1.at[slot], r1.at[slot], device(*there))
-                two = send(ls.at[tc, h], x0.at[:, slot, :, to_half], s2.at[slot], r2.at[slot], device(*there))
-            two.start()
-            one.start()
-            copies.append(one)
-            leads.append((i, slot, two))
-
-    def grad_piece(t):
-        return grad.at[pl.ds(pl.multiple_of(t * 32, 32), 32)]
-
-    def lead_piece(t):
-        return b0.at[pl.ds(pl.multiple_of(t * 16, 16), 16)]
+    mask(0)
+    to_self = jnp.where(is_me((to_d, mine)), 1, 0) + jnp.where(is_me((to_d, mine + 16)), 1, 0)
+    lead_self = jnp.where(is_me(lead_target(f)), 1, 0)
+    pl.semaphore_wait(barrier, 29 + 15 + 31 + 3 + 2 - to_self + jnp.where(mine == 0, 32 - lead_self, 0))
+    tokens = [exchange(0)]
+    mask(1)
+    tokens.append(exchange(1))
 
     @pl.when(f == 0)
     def _():
@@ -153,90 +236,22 @@
             send(grad_piece(t), piece_g, s3.at[t], r3.at[0], (d, t)).start()
             send(lead_piece(t), piece_b, s4.at[t], r3.at[1], (d, t)).start()
 
-    passed = []
-    for i, slot, two in leads:
-        mine = x0.at[:, slot, :, half]
-        arrived(mine, r2.at[slot])
-        on = send(mine, x0.at[:, slot ^ 1, :, half], s5.at[slot], r4.at[slot ^ 1], partner)
-        on.start()
-        passed.append(on)
-    for i, slot, two in leads:
-        if i > 0:
-            two.wait_send()
-    for slot, on in zip([slot for _, slot, _ in leads], passed):
-        on.wait_send()
-        arrived(x0.at[:, slot, :, other_half], r4.at[slot])
-    for one in copies:
-        one.wait()
-    arrived(piece_g, r3.at[0])
-    arrived(piece_b, r3.at[1])
-
-    @pl.when(f == 0)
-    def _():
-        @pl.loop(1, 32)
-        def _(t):
-            send(grad_piece(t), piece_g, s3.at[t], r3.at[0], (d, t)).wait_send()
-            send(lead_piece(t), piece_b, s4.at[t], r3.at[1], (d, t)).wait_send()
-
-
-def dot(a, b):
-    return jnp.dot(a, b, precision=highest, preferred_element_type=f32)
-
-
-def dot16(a, b):
-    return jnp.dot(a, b, preferred_element_type=f32)
-
-
-def stats_body(
-    xc, x0, k_factor, c_factor, piece_b, piece_g, h_out, u_out, gram_out, tr_out, b0_out, g0_out,
-    ps, pi, sm, st, tr, lead_b, lead_g,
-    rs_s, rs_r, de_s, de_r, ag_s, zb_s, zb_r, zg_s, zg_r, xb_s, xb_r, xg_s, xg_r, tr_s, tr_r,
-):
-    x, y, z, c = position()
-    d, f = lax.axis_index("dp"), lax.axis_index("fsdp")
-    barrier = pltpu.get_barrier_semaphore()
-    mine = class_of(x, y, z, c)
-    xi, yi, zi = lax.div(x, 2), lax.div(y, 2), lax.div(z, 2)
-    slot = xi * 8 + yi * 4 + zi
-    mates = [(a, b, g) for a in range(2) for b in range(2) for g in range(4)]
-
-    def mate(a, b, g):
-        return lax.rem(x + 2 * a, NX), lax.rem(y + 2 * b, NY), lax.rem(z + 2 * g, NZ)
-
-    to_d = lax.rem(y + lax.rem(zi, 2), NY) * 2 + lax.div(zi, 2)
-    k = lax.rem(f, 16)
-    px, py, pc, pz = lax.div(k, 8), lax.rem(lax.div(k, 4), 2), lax.rem(lax.div(k, 2), 2), lax.rem(k, 2)
-    shift = lax.rem(y + py, 2)
-    from_y = lax.rem(y - shift + NY, NY)
-    from_zi = 2 * c + shift
-    from_j = [i * 8 + lax.div(from_y, 2) * 4 + from_zi for i in range(2)]
-    from_at = [device(px + 2 * i, from_y, pz + 2 * from_zi, pc) for i in range(2)]
-
-    def is_me(there):
-        return jnp.logical_and(there[0] == d, there[1] == f)
-
-    for o in mates[1:]:
-        greet(barrier, device(*mate(*o), c))
-
-    @pl.loop(1, 32)
-    def _(t):
-        greet(barrier, (d, lax.rem(f + t, 32)))
-
-    for t in range(1, 8):
-        greet(barrier, (lax.rem(d + t, 8), f))
-    for there in from_at:
-
-        @pl.when(jnp.logical_not(is_me(there)))
-        def _():
-            greet(barrier, there)
+    flag = jnp.where(f > 0, 1.0, 0.0)
+    for side, factor in enumerate((k_factor, c_factor)):
+        diag = factor[0, :, 0:256]
+        border = factor[0, :, 256:512] * flag
+        gram_out[side] = dot(diag.T, diag) + dot(border.T, border)
+        tr_g = jnp.sum(diag * diag) + jnp.sum(border * border)
+        tr[f, side * 2 + 1 : side * 2 + 2, :] = jnp.full((1, 128), tr_g, f32)
+    tr[f, 4:8, :] = jnp.zeros((4, 128), f32)
 
     dims = (((0,), (0,)), ((), ()))
 
     def gram(side):
-        lead = x0[side]
-        a = xc[side, :, 0:256]
-        b = xc[side, :, 256:512]
-        for i, (left, right) in enumerate(((a, a), (b, b), (lead, a), (lead, b), (lead, lead))):
+        lead = x0[side].reshape(2048, 256)
+        a = xc[side, :, :, 0:256].reshape(2048, 256)
+        b = xc[side, :, :, 256:512].reshape(2048, 256)
+        for i, (left, right) in enumerate(((a, a), (b, b), (lead, a), (lead, b))):
             g = lax.dot_general(left, right, dims, preferred_element_type=f32)
             ps[side, :, i, :, :] = g.astype(bf16).reshape(16, 16, 256)
 
@@ -251,10 +266,15 @@
                 copies.append(copy)
         return copies
 
+    passed = collect(0, tokens[0])
     gram(0)
-    to_self = jnp.where(is_me((to_d, mine)), 1, 0) + jnp.where(is_me((to_d, mine + 16)), 1, 0)
-    pl.semaphore_wait(barrier, 15 + 31 + 7 + 2 - to_self)
-    first = scatter(0)
+    sums = [scatter(0)]
+    passed += collect(1, tokens[1])
+    gram(1)
+    sums.append(scatter(1))
+
+    arrived(piece_g, r3.at[0])
+    arrived(piece_b, r3.at[1])
     own_b = pltpu.make_async_copy(piece_b, lead_b.at[x, z], zb_r.at[0])
     own_g = pltpu.make_async_copy(piece_g, lead_g.at[x, z], zg_r.at[0])
     own_b.start()
@@ -263,49 +283,75 @@
         there = (d, x * NZ + lax.rem(z + t, NZ))
         send(piece_b, lead_b.at[x, z], zb_s.at[t], zb_r.at[t], there).start()
         send(piece_g, lead_g.at[x, z], zg_s.at[t], zg_r.at[t], there).start()
-    gram(1)
-    second = scatter(1)
-
-    flag = jnp.where(f > 0, 1.0, 0.0)
-    factors = []
-    for side, factor in enumerate((k_factor, c_factor)):
-        diag = factor[0, :, 0:256]
-        border = factor[0, :, 256:512] * flag
-        gram_out[side] = dot(diag.T, diag) + dot(border.T, border)
-        factors.append((diag, border))
-
-    def total(side, copies):
-        for copy in copies:
+
+    def total(side):
+        for copy in sums[side]:
             copy.wait()
         value = ps[side, slot].astype(f32)
         for i in range(1, 16):
             value = value + pi[side, i].astype(f32)
         value = value.astype(bf16)
         for m in range(2):
-            for q, source in enumerate((m, 2 + m, 4)):
-                sm[side, m, q] = value[source]
+            for q in range(2):
+                sm[side, m, q] = value[2 * q + m]
+
+    def lead_send(side, t):
+        return send(sm.at[side, 0, 0], st.at[side, slot, 2], a0_s.at[side, t], a0_r.at[side, slot], lead_target(t))
+
+    def rows_send(side, m):
+        there = (to_d, mine + 16 * m)
+        return send(sm.at[side, m], st.at[side, slot, 0:2], de_s.at[side, m], de_r.at[side, slot], there)
 
     def deliver(side):
+        @pl.when(mine == 0)
+        def _():
+            @pl.loop(0, 32)
+            def _(t):
+                me = is_me(lead_target(t))
+
+                @pl.when(me)
+                def _():
+                    pltpu.make_async_copy(sm.at[side, 0, 0], st.at[side, slot, 2], a0_r.at[side, slot]).start()
+
+                @pl.when(jnp.logical_not(me))
+                def _():
+                    lead_send(side, t).start()
+
         for m in range(2):
-            there = (to_d, mine + 16 * m)
-
-            @pl.when(is_me(there))
+            me = is_me((to_d, mine + 16 * m))
+
+            @pl.when(me)
             def _():
-                pltpu.make_async_copy(sm.at[side, m], st.at[side, slot], de_r.at[side, slot]).start()
-
-            @pl.when(jnp.logical_not(is_me(there)))
+                pltpu.make_async_copy(sm.at[side, m], st.at[side, slot, 0:2], de_r.at[side, slot]).start()
+
+            @pl.when(jnp.logical_not(me))
             def _():
-                send(sm.at[side, m], st.at[side, slot], de_s.at[side, m], de_r.at[side, slot], there).start()
+                rows_send(side, m).start()
+
+    def share_send(side, i, t):
+        there = device(x, lax.rem(y + t, NY), z, c) if t > 0 else partner
+        at = st.at[side, from_j[i]]
+        return send(at, at, ag_s.at[side, i, t], de_r.at[side, from_j[i]], there)
+
+    def pass_send(side, i, t):
+        j = slots_at(lax.rem(y + NY - t, NY))[i]
+        return send(st.at[side, j], st.at[side, j], fw_s.at[side, i, t], de_r.at[side, j], partner)
 
     def share(side):
         for i in range(2):
-            j = from_j[i]
-            arrived(st.at[side, j], de_r.at[side, j])
-            for t in range(1, 8):
-                there = (lax.rem(d + t, 8), f)
-                send(st.at[side, j], st.at[side, j], ag_s.at[side, i, t], de_r.at[side, j], there).start()
-
-    total(0, first)
+            arrived(st.at[side, from_j[i], 0:2], de_r.at[side, from_j[i]])
+            arrived(st.at[side, from_j[i], 2], a0_r.at[side, from_j[i]])
+            for t in (1, 2, 3, 0):
+                share_send(side, i, t).start()
+
+    def pass_on(side):
+        for t in (1, 3, 2):
+            for i in range(2):
+                j = slots_at(lax.rem(y + NY - t, NY))[i]
+                arrived(st.at[side, j], de_r.at[side, j])
+                pass_send(side, i, t).start()
+
+    total(0)
     deliver(0)
     own_b.wait()
     own_g.wait()
@@ -316,9 +362,10 @@
         send(piece_g, lead_g.at[x, z], zg_s.at[t], zg_r.at[t], there).wait_send()
         arrived(lead_b.at[x, behind], zb_r.at[t])
         arrived(lead_g.at[x, behind], zg_r.at[t])
-    total(1, second)
+    share(0)
+    total(1)
     deliver(1)
-    share(0)
+    pass_on(0)
     share(1)
     for t in range(1, 4):
         there = (d, lax.rem(x + t, NX) * NZ + z)
@@ -327,28 +374,29 @@
 
     rows = lax.broadcasted_iota(jnp.int32, (256, 256), 0)
     cols = lax.broadcasted_iota(jnp.int32, (256, 256), 1)
-    for side, (diag, border) in enumerate(factors):
+
+    def second_moment(side):
         for j in range(16):
-            mine_too = jnp.logical_or(from_j[0] == j, from_j[1] == j)
-
-            @pl.when(jnp.logical_not(mine_too))
+            @pl.when(lax.div(j % 4, 2) != c)
             def _():
                 arrived(st.at[side, j], de_r.at[side, j])
 
+        factor = (k_factor, c_factor)[side]
+        diag16 = factor[0, :, 0:256].astype(bf16)
+        border16 = (factor[0, :, 256:512] * flag).astype(bf16)
         a = st[side, :, 0].reshape(256, 256)
         cross = st[side, :, 1].reshape(256, 256)
         lead = st[side, :, 2].reshape(256, 256)
-        diag16, border16 = diag.astype(bf16), border.astype(bf16)
         u = dot16(cross, diag16) + dot16(lead, border16)
         v = dot16(a, diag16) + dot16(cross.T, border16)
         h = dot(diag16.astype(f32).T, v) + dot(border16.astype(f32).T, u)
         u_out[side] = u
         h_out[side] = h
-        tr_h = jnp.sum(jnp.where(rows == cols, h, 0.0))
-        tr_g = jnp.sum(diag * diag) + jnp.sum(border * border)
-        tr[f, side * 2 : side * 2 + 1, :] = jnp.full((1, 128), tr_h, f32)
-        tr[f, side * 2 + 1 : side * 2 + 2, :] = jnp.full((1, 128), tr_g, f32)
-    tr[f, 4:8, :] = jnp.zeros((4, 128), f32)
+        tr[f, side * 2 : side * 2 + 1, :] = jnp.full((1, 128), jnp.sum(jnp.where(rows == cols, h, 0.0)), f32)
+
+    second_moment(0)
+    pass_on(1)
+    second_moment(1)
 
     @pl.loop(1, 32)
     def _(t):
@@ -363,29 +411,52 @@
         arrived(lead_g.at[behind], xg_r.at[t])
     b0_out[...] = lead_b[...].reshape(512, 256)
     g0_out[...] = lead_g[...].reshape(1024, 256)
+    for on in passed:
+        on.wait_send()
+    for copies in tokens:
+        for i, at, one, two in copies:
+            if i > 0:
+                one.wait_send()
+                two.wait_send()
+
+    @pl.when(f == 0)
+    def _():
+        @pl.loop(1, 32)
+        def _(t):
+            send(grad_piece(t), piece_g, s3.at[t], r3.at[0], (d, t)).wait_send()
+            send(lead_piece(t), piece_b, s4.at[t], r3.at[1], (d, t)).wait_send()
+
     for side in range(2):
+
+        @pl.when(mine == 0)
+        def _():
+            @pl.loop(0, 32)
+            def _(t):
+                @pl.when(jnp.logical_not(is_me(lead_target(t))))
+                def _():
+                    lead_send(side, t).wait_send()
+
         for m in range(2):
-            there = (to_d, mine + 16 * m)
-
-            @pl.when(jnp.logical_not(is_me(there)))
+
+            @pl.when(jnp.logical_not(is_me((to_d, mine + 16 * m))))
             def _():
-                send(sm.at[side, m], st.at[side, slot], de_s.at[side, m], de_r.at[side, slot], there).wait_send()
+                rows_send(side, m).wait_send()
 
         for i in range(2):
-            j = from_j[i]
-            for t in range(1, 8):
-                there = (lax.rem(d + t, 8), f)
-                send(st.at[side, j], st.at[side, j], ag_s.at[side, i, t], de_r.at[side, j], there).wait_send()
+            for t in range(4):
+                share_send(side, i, t).wait_send()
+            for t in range(1, 4):
+                pass_send(side, i, t).wait_send()
 
     @pl.loop(1, 32)
     def _(t):
         send(tr.at[f], tr.at[f], tr_s.at[t], tr_r.at[t], (d, lax.rem(f + t, 32))).wait_send()
         arrived(tr.at[lax.rem(f + 32 - t, 32)], tr_r.at[t])
 
-    sums = tr[0]
+    result = tr[0]
     for i in range(1, 32):
-        sums = sums + tr[i]
-    tr_out[...] = sums
+        result = result + tr[i]
+    tr_out[...] = result
 
 
 def advance_body(
@@ -590,22 +661,18 @@
 def per_device(acts, out_grads, token_counts, k_factor, c_factor, k_moment, c_moment, grad_weight):
     SM = pl.BlockSpec(memory_space=pltpu.SMEM)
     V = pltpu.VMEM
-    xc, x0, piece_b, piece_g = call(
-        token_body, "tokens", (token_counts, acts, out_grads, k_factor, c_factor, grad_weight), [SM] + [VM] * 5,
-        [((2, 32, 64, 512), bf16), ((2, 32, 64, 256), bf16), ((16, 256), bf16), ((32, 256), bf16)], [ANY] * 4,
-        [V((16, 2, 2, 64, 512), bf16), V((2, 2, 2, 64, 128), bf16), V((512, 256), bf16)]
-        + [DMA((32,))] * 5 + [DMA((2,)), DMA((2,)), DMA((32,)), DMA((32,)), DMA((32,))],
-        0,
-    )
     h, u, grams, traces, leads, grad_lead = call(
         stats_body, "stats",
-        (xc.reshape(2, 2048, 512), x0.reshape(2, 2048, 256), k_factor, c_factor, piece_b, piece_g),
-        [VM] * 4 + [ANY] * 2,
+        (token_counts, acts, out_grads, k_factor, c_factor, grad_weight), [SM, ANY, ANY, VM, VM, ANY],
         [((2, 256, 256), f32)] * 3 + [((8, 128), f32), ((512, 256), bf16), ((1024, 256), bf16)], [VM] * 6,
-        [V((2, 16, 5, 16, 256), bf16), V((2, 16, 5, 16, 256), bf16), V((2, 2, 3, 16, 256), bf16),
+        [V((2, 128, 8192), bf16), V((2, 16, 2, 64, 512), bf16), V((2, 2, 2, 64, 128), bf16),
+         V((2, 32, 64, 512), bf16), V((2, 32, 64, 256), bf16), V((512, 256), bf16), V((16, 256), bf16),
+         V((32, 256), bf16), V((2, 16, 4, 16, 256), bf16), V((2, 16, 4, 16, 256), bf16), V((2, 2, 2, 16, 256), bf16),
          V((2, 16, 3, 16, 256), bf16), V((32, 8, 128), f32), V((4, 8, 16, 256), bf16), V((4, 8, 32, 256), bf16),
-         DMA((2, 16)), DMA((2, 16)), DMA((2, 2)), DMA((2, 16)), DMA((2, 2, 8)), DMA((8,)), DMA((8,)), DMA((8,)),
-         DMA((8,)), DMA((4,)), DMA((4,)), DMA((4,)), DMA((4,)), DMA((32,)), DMA((32,))],
+         DMA((2,))] + [DMA((2, 32))] * 6 + [DMA((32,)), DMA((32,)), DMA((2,)),
+         DMA((2, 16)), DMA((2, 16)), DMA((2, 2)), DMA((2, 16)), DMA((2, 32)), DMA((2, 16)), DMA((2, 2, 4)),
+         DMA((2, 2, 4)), DMA((8,)), DMA((8,)), DMA((8,)), DMA((8,)), DMA((4,)), DMA((4,)), DMA((4,)), DMA((4,)),
+         DMA((32,)), DMA((32,))],
         1,
     )
     k_new, c_new, km_new, cm_new, k_half, c_half = call(

time: 185 us -> 170 us (0.919)
  Pallas kernels: 182 us -> 167 us
    pallas_call x4 -> x3, Pallas kernels: 182 us -> 167 us  [call(): pl.pallas_call(body, out_shape=[jax.ShapeDtypeStruct(s, t) for s, t in ou...]
where the time goes in v3:
time: 170 us
  Pallas kernels  167 us (98%)
  local copies, waits for them, and re-layouts  1.87 us (1%)
    pallas_call x3, Pallas kernels, call(): pl.pallas_call(body, out_shape=[jax.ShapeDtypeStruct(s, t) for s, t in ou...  167 us

profile of v3, /device:TPU:0, one launch (start us, length us, event | category | flops | bytes accessed | tf_op | source)
XLA Modules:
  0.0 169.7 jit_solution(2541864985361300463)
XLA Ops:
  0.6 109.8 %stats.1 = (f32[2,256,256]{2,1,0:T(8,128)}, f32[2,256,256]{2,1,0:T(8,128)}, f32[2,256,256]{2,1,0:T(8,128)}, f32[8,128]{1,0:T(8,128)}, bf16[512,256]{1,0:T(8,128)(2,1)}, /*index=5*/bf16[1024,256]{1,0:T(8,128)(2,1)}) custom-call(s32[8]{0:T(128)} %counts.3, bf16[128,8192]{1,0:T(8,128)(2,1)} %acts.1, bf16[128,8192]{1,0:T(8,128)(2,1)} %grads.1, ...), custom_call_target="tpu_custom_call" | custom-call | tf_op jit(solution)/shard_map/stats/pallas_call | solution.py:57
  110.4 5.5 %advance.1 = (f32[1,256,512]{2,1,0:T(8,128)}, f32[1,256,512]{2,1,0:T(8,128)}, f32[1,256,512]{2,1,0:T(8,128)}, f32[1,256,512]{2,1,0:T(8,128)}, bf16[512,256]{1,0:T(8,128)(2,1)}, /*index=5*/bf16[512,256]{1,0:T(8,128)(2,1)}) custom-call(s32[8]{0:T(128)} %counts.3, f32[8,128]{1,0:T(8,128)} %get-tuple-element.17.traces, f32[2,256,256]{2,1,0:T(8,128)} %get-tuple-element.18.h_in, ...), custom_call_target="tpu_custom_call" | custom-call | tf_op jit(solution)/shard_map/advance/pallas_call | solution.py:57
  115.9 52.0 %precond.1 = bf16[1024,256]{1,0:T(8,128)(2,1)} custom-call(bf16[512,256]{1,0:T(8,128)(2,1)} %get-tuple-element.26.k_half, bf16[512,256]{1,0:T(8,128)(2,1)} %get-tuple-element.27.c_half, bf16[1024,256]{1,0:T(8,128)(2,1)} %grad.3, bf16[1024,256]{1,0:T(8,128)(2,1)} %get-tuple-element.28.grad_lead), custom_call_target="tpu_custom_call" | custom-call | tf_op jit(solution)/shard_map/precond/pallas_call | solution.py:57
  167.9 1.9 %copy.14 = bf16[1024,256]{1,0:T(8,128)(2,1)} copy(bf16[1024,256]{1,0:T(8,128)(2,1)} %precond.1) | data formatting | bytes 1048576

commit v4 on v3

--- a/solution.py
+++ b/solution.py
@@ -73,11 +73,21 @@
     return jnp.dot(a, b, preferred_element_type=f32)
 
 
-def stats_body(
-    counts, acts, grads, k_factor, c_factor, grad, h_out, u_out, gram_out, tr_out, b0_out, g0_out,
-    raw, xs, ls, xc, x0, b0, piece_b, piece_g, ps, pi, sm, st, tr, lead_b, lead_g,
+def dot(a, b):
+    return jnp.dot(a, b, precision=highest, preferred_element_type=f32)
+
+
+def dot16(a, b):
+    return jnp.dot(a, b, preferred_element_type=f32)
+
+
+def step_body(
+    counts, acts, grads, k_factor, c_factor, k_moment, c_moment, grad, k_new, c_new, km_new, cm_new, out,
+    h_out, u_out, gram_out, lead_src, lead_in, own, lead_sum, all_lead, second, lead_rows, cb, term, terms, part, k_half,
+    c_half, raw, xs, ls, xc, x0, b0, piece_b, piece_g, ps, py_in, qx, px_in, qz, pz_in, sm, st, tr, lead_b, lead_g,
     in_s, s1, r1, s2, r2, s5, r4, s3, s4, r3,
     rs_s, rs_r, de_s, de_r, a0_s, a0_r, ag_s, fw_s, zb_s, zb_r, zg_s, zg_r, xb_s, xb_r, xg_s, xg_r, tr_s, tr_r,
+    bo_s, bo_r, ga_s, ga_r, ca_s, ca_r, cz_s, cz_r, cx_s, cx_r, ro_s, ro_r, te_s, te_r,
 ):
     x, y, z, c = position()
     d, f = lax.axis_index("dp"), lax.axis_index("fsdp")
@@ -98,11 +108,12 @@
     offsets = [(a, b, g, e) for a in (0, 1) for b in (0, 1) for g in (0, 1) for e in (0, 1)]
     mine = class_of(x, y, z, c)
     xi, yi, zi = lax.div(x, 2), lax.div(y, 2), lax.div(z, 2)
-    slot = xi * 8 + yi * 4 + zi
-    mates = [(a, b, g) for a in range(2) for b in range(2) for g in range(4)]
-
-    def mate(a, b, g):
-        return lax.rem(x + 2 * a, NX), lax.rem(y + 2 * b, NY), lax.rem(z + 2 * g, NZ)
+    slot = yi * 8 + xi * 4 + zi
+    mate_y = device(x, lax.rem(y + 2, NY), z, c)
+    mate_x = device(lax.rem(x + 2, NX), y, z, c)
+
+    def mate_z(g):
+        return device(x, y, lax.rem(z + 2 * g, NZ), c)
 
     k = lax.rem(f, 16)
     px, py, pc, pz = lax.div(k, 8), lax.rem(lax.div(k, 4), 2), lax.rem(lax.div(k, 2), 2), lax.rem(k, 2)
@@ -112,11 +123,11 @@
 
     def slots_at(there_y):
         shift = lax.rem(there_y + py, 2)
-        low = lax.div(lax.rem(there_y - shift + NY, NY), 2) * 4 + 2 * c + shift
-        return [low, low + 8]
+        low = lax.div(lax.rem(there_y - shift + NY, NY), 2) * 8 + 2 * c + shift
+        return [low, low + 4]
 
     def owner(j, qx, qy, qz, qc):
-        return device(qx + 2 * lax.div(j, 8), qy + 2 * lax.rem(lax.div(j, 4), 2), qz + 2 * lax.rem(j, 4), qc)
+        return device(qx + 2 * lax.rem(lax.div(j, 4), 2), qy + 2 * lax.div(j, 8), qz + 2 * lax.rem(j, 4), qc)
 
     to_d = group_for(lax.rem(y, 2))
     from_j = slots_at(y)
@@ -132,8 +143,8 @@
             if o[:3] == (0, 0, 0) and (o[3] == 0 or sign == -1):
                 continue
             greet(barrier, device(*cell(sign, *o)))
-    for o in mates[1:]:
-        greet(barrier, device(*mate(*o), c))
+    for there in (mate_y, mate_x, mate_z(1), mate_z(2), mate_z(3)):
+        greet(barrier, there)
 
     @pl.loop(1, 32)
     def _(t):
@@ -147,6 +158,15 @@
             @pl.when(jnp.logical_not(is_me(there)))
             def _():
                 greet(barrier, there)
+
+    @pl.when(d == 0)
+    def _():
+        for t in range(1, 8):
+            greet(barrier, (t, f))
+
+    @pl.when(d > 0)
+    def _():
+        greet(barrier, (0, f))
 
     limit = counts[0] * jnp.where(d == 0, 1, 0)
     for i in range(1, 8):
@@ -221,7 +241,9 @@
     mask(0)
     to_self = jnp.where(is_me((to_d, mine)), 1, 0) + jnp.where(is_me((to_d, mine + 16)), 1, 0)
     lead_self = jnp.where(is_me(lead_target(f)), 1, 0)
-    pl.semaphore_wait(barrier, 29 + 15 + 31 + 3 + 2 - to_self + jnp.where(mine == 0, 32 - lead_self, 0))
+    pl.semaphore_wait(
+        barrier, 29 + 5 + 31 + 3 + 2 - to_self + jnp.where(mine == 0, 32 - lead_self, 0) + jnp.where(d == 0, 7, 1)
+    )
     tokens = [exchange(0)]
     mask(1)
     tokens.append(exchange(1))
@@ -235,6 +257,7 @@
         def _(t):
             send(grad_piece(t), piece_g, s3.at[t], r3.at[0], (d, t)).start()
             send(lead_piece(t), piece_b, s4.at[t], r3.at[1], (d, t)).start()
+
 
     flag = jnp.where(f > 0, 1.0, 0.0)
     for side, factor in enumerate((k_factor, c_factor)):
@@ -255,24 +278,102 @@
             g = lax.dot_general(left, right, dims, preferred_element_type=f32)
             ps[side, :, i, :, :] = g.astype(bf16).reshape(16, 16, 256)
 
-    def scatter(side):
-        copies = []
-        for i, o in enumerate(mates):
-            if i > 0:
-                tx, ty, tz = mate(*o)
-                j = lax.div(tx, 2) * 8 + lax.div(ty, 2) * 4 + lax.div(tz, 2)
-                copy = send(ps.at[side, j], pi.at[side, i], rs_s.at[side, i], rs_r.at[side, i], device(tx, ty, tz, c))
-                copy.start()
-                copies.append(copy)
-        return copies
+    def y_copy(side):
+        src = ps.at[side, pl.ds((1 - yi) * 8, 8)]
+        return send(src, py_in.at[side], rs_s.at[side, 0], rs_r.at[side, 0], mate_y)
+
+    def x_copy(side):
+        src = qx.at[side, pl.ds((1 - xi) * 4, 4)]
+        return send(src, px_in.at[side], rs_s.at[side, 1], rs_r.at[side, 1], mate_x)
+
+    def z_copy(side, g):
+        src = qz.at[side, lax.rem(zi + g, 4)]
+        return send(src, pz_in.at[side, g], rs_s.at[side, 1 + g], rs_r.at[side, 1 + g], mate_z(g))
+
+    def over_x(side):
+        arrived(py_in.at[side], rs_r.at[side, 0])
+        qx[side] = (ps[side, pl.ds(yi * 8, 8)].astype(f32) + py_in[side].astype(f32)).astype(bf16)
+        x_copy(side).start()
+
+    def over_z(side):
+        arrived(px_in.at[side], rs_r.at[side, 1])
+        qz[side] = (qx[side, pl.ds(xi * 4, 4)].astype(f32) + px_in[side].astype(f32)).astype(bf16)
+        for g in range(1, 4):
+            z_copy(side, g).start()
 
     passed = collect(0, tokens[0])
     gram(0)
-    sums = [scatter(0)]
+    y_copy(0).start()
     passed += collect(1, tokens[1])
     gram(1)
-    sums.append(scatter(1))
-
+    y_copy(1).start()
+    def total(side):
+        value = qz[side, zi].astype(f32)
+        for g in range(1, 4):
+            arrived(pz_in.at[side, g], rs_r.at[side, 1 + g])
+            value = value + pz_in[side, g].astype(f32)
+        value = value.astype(bf16)
+        for m in range(2):
+            for q in range(2):
+                sm[side, m, q] = value[2 * q + m]
+
+    def lead_send(side, t):
+        return send(sm.at[side, 0, 0], st.at[side, slot, 2], a0_s.at[side, t], a0_r.at[side, slot], lead_target(t))
+
+    def rows_send(side, m):
+        there = (to_d, mine + 16 * m)
+        return send(sm.at[side, m], st.at[side, slot, 0:2], de_s.at[side, m], de_r.at[side, slot], there)
+
+    def deliver(side):
+        @pl.when(mine == 0)
+        def _():
+            @pl.loop(0, 32)
+            def _(t):
+                me = is_me(lead_target(t))
+
+                @pl.when(me)
+                def _():
+                    pltpu.make_async_copy(sm.at[side, 0, 0], st.at[side, slot, 2], a0_r.at[side, slot]).start()
+
+                @pl.when(jnp.logical_not(me))
+                def _():
+                    lead_send(side, t).start()
+
+        for m in range(2):
+            me = is_me((to_d, mine + 16 * m))
+
+            @pl.when(me)
+            def _():
+                pltpu.make_async_copy(sm.at[side, m], st.at[side, slot, 0:2], de_r.at[side, slot]).start()
+
+            @pl.when(jnp.logical_not(me))
+            def _():
+                rows_send(side, m).start()
+
+    def share_send(side, i, t):
+        there = device(x, lax.rem(y + t, NY), z, c) if t > 0 else partner
+        at = st.at[side, from_j[i]]
+        return send(at, at, ag_s.at[side, i, t], de_r.at[side, from_j[i]], there)
+
+    def pass_send(side, i, t):
+        j = slots_at(lax.rem(y + NY - t, NY))[i]
+        return send(st.at[side, j], st.at[side, j], fw_s.at[side, i, t], de_r.at[side, j], partner)
+
+    def share(side):
+        for i in range(2):
+            arrived(st.at[side, from_j[i], 0:2], de_r.at[side, from_j[i]])
+            arrived(st.at[side, from_j[i], 2], a0_r.at[side, from_j[i]])
+            for t in (1, 2, 3, 0):
+                share_send(side, i, t).start()
+
+    def pass_on(side):
+        for t in (1, 3, 2):
+            for i in range(2):
+                j = slots_at(lax.rem(y + NY - t, NY))[i]
+                arrived(st.at[side, j], de_r.at[side, j])
+                pass_send(side, i, t).start()
+
+    over_x(0)
     arrived(piece_g, r3.at[0])
     arrived(piece_b, r3.at[1])
     own_b = pltpu.make_async_copy(piece_b, lead_b.at[x, z], zb_r.at[0])
@@ -283,76 +384,13 @@
         there = (d, x * NZ + lax.rem(z + t, NZ))
         send(piece_b, lead_b.at[x, z], zb_s.at[t], zb_r.at[t], there).start()
         send(piece_g, lead_g.at[x, z], zg_s.at[t], zg_r.at[t], there).start()
-
-    def total(side):
-        for copy in sums[side]:
-            copy.wait()
-        value = ps[side, slot].astype(f32)
-        for i in range(1, 16):
-            value = value + pi[side, i].astype(f32)
-        value = value.astype(bf16)
-        for m in range(2):
-            for q in range(2):
-                sm[side, m, q] = value[2 * q + m]
-
-    def lead_send(side, t):
-        return send(sm.at[side, 0, 0], st.at[side, slot, 2], a0_s.at[side, t], a0_r.at[side, slot], lead_target(t))
-
-    def rows_send(side, m):
-        there = (to_d, mine + 16 * m)
-        return send(sm.at[side, m], st.at[side, slot, 0:2], de_s.at[side, m], de_r.at[side, slot], there)
-
-    def deliver(side):
-        @pl.when(mine == 0)
-        def _():
-            @pl.loop(0, 32)
-            def _(t):
-                me = is_me(lead_target(t))
-
-                @pl.when(me)
-                def _():
-                    pltpu.make_async_copy(sm.at[side, 0, 0], st.at[side, slot, 2], a0_r.at[side, slot]).start()
-
-                @pl.when(jnp.logical_not(me))
-                def _():
-                    lead_send(side, t).start()
-
-        for m in range(2):
-            me = is_me((to_d, mine + 16 * m))
-
-            @pl.when(me)
-            def _():
-                pltpu.make_async_copy(sm.at[side, m], st.at[side, slot, 0:2], de_r.at[side, slot]).start()
-
-            @pl.when(jnp.logical_not(me))
-            def _():
-                rows_send(side, m).start()
-
-    def share_send(side, i, t):
-        there = device(x, lax.rem(y + t, NY), z, c) if t > 0 else partner
-        at = st.at[side, from_j[i]]
-        return send(at, at, ag_s.at[side, i, t], de_r.at[side, from_j[i]], there)
-
-    def pass_send(side, i, t):
-        j = slots_at(lax.rem(y + NY - t, NY))[i]
-        return send(st.at[side, j], st.at[side, j], fw_s.at[side, i, t], de_r.at[side, j], partner)
-
-    def share(side):
-        for i in range(2):
-            arrived(st.at[side, from_j[i], 0:2], de_r.at[side, from_j[i]])
-            arrived(st.at[side, from_j[i], 2], a0_r.at[side, from_j[i]])
-            for t in (1, 2, 3, 0):
-                share_send(side, i, t).start()
-
-    def pass_on(side):
-        for t in (1, 3, 2):
-            for i in range(2):
-                j = slots_at(lax.rem(y + NY - t, NY))[i]
-                arrived(st.at[side, j], de_r.at[side, j])
-                pass_send(side, i, t).start()
-
+    over_x(1)
+    over_z(0)
+    over_z(1)
     total(0)
     deliver(0)
+    total(1)
+    deliver(1)
     own_b.wait()
     own_g.wait()
     for t in range(1, 8):
@@ -362,15 +400,14 @@
         send(piece_g, lead_g.at[x, z], zg_s.at[t], zg_r.at[t], there).wait_send()
         arrived(lead_b.at[x, behind], zb_r.at[t])
         arrived(lead_g.at[x, behind], zg_r.at[t])
-    share(0)
-    total(1)
-    deliver(1)
-    pass_on(0)
-    share(1)
     for t in range(1, 4):
         there = (d, lax.rem(x + t, NX) * NZ + z)
         send(lead_b.at[x], lead_b.at[x], xb_s.at[t], xb_r.at[t], there).start()
         send(lead_g.at[x], lead_g.at[x], xg_s.at[t], xg_r.at[t], there).start()
+    share(0)
+    share(1)
+    pass_on(0)
+    pass_on(1)
 
     rows = lax.broadcasted_iota(jnp.int32, (256, 256), 0)
     cols = lax.broadcasted_iota(jnp.int32, (256, 256), 1)
@@ -395,7 +432,6 @@
         tr[f, side * 2 : side * 2 + 1, :] = jnp.full((1, 128), jnp.sum(jnp.where(rows == cols, h, 0.0)), f32)
 
     second_moment(0)
-    pass_on(1)
     second_moment(1)
 
     @pl.loop(1, 32)
@@ -409,81 +445,33 @@
         send(lead_g.at[x], lead_g.at[x], xg_s.at[t], xg_r.at[t], there).wait_send()
         arrived(lead_b.at[behind], xb_r.at[t])
         arrived(lead_g.at[behind], xg_r.at[t])
-    b0_out[...] = lead_b[...].reshape(512, 256)
-    g0_out[...] = lead_g[...].reshape(1024, 256)
-    for on in passed:
-        on.wait_send()
-    for copies in tokens:
-        for i, at, one, two in copies:
-            if i > 0:
-                one.wait_send()
-                two.wait_send()
-
-    @pl.when(f == 0)
-    def _():
-        @pl.loop(1, 32)
-        def _(t):
-            send(grad_piece(t), piece_g, s3.at[t], r3.at[0], (d, t)).wait_send()
-            send(lead_piece(t), piece_b, s4.at[t], r3.at[1], (d, t)).wait_send()
-
-    for side in range(2):
-
-        @pl.when(mine == 0)
-        def _():
-            @pl.loop(0, 32)
-            def _(t):
-                @pl.when(jnp.logical_not(is_me(lead_target(t))))
-                def _():
-                    lead_send(side, t).wait_send()
-
-        for m in range(2):
-
-            @pl.when(jnp.logical_not(is_me((to_d, mine + 16 * m))))
-            def _():
-                rows_send(side, m).wait_send()
-
-        for i in range(2):
-            for t in range(4):
-                share_send(side, i, t).wait_send()
-            for t in range(1, 4):
-                pass_send(side, i, t).wait_send()
 
     @pl.loop(1, 32)
     def _(t):
         send(tr.at[f], tr.at[f], tr_s.at[t], tr_r.at[t], (d, lax.rem(f + t, 32))).wait_send()
         arrived(tr.at[lax.rem(f + 32 - t, 32)], tr_r.at[t])
 
-    result = tr[0]
+    sums_all = tr[0]
     for i in range(1, 32):
-        result = result + tr[i]
-    tr_out[...] = result
-
-
-def advance_body(
-    counts, traces, h_in, u_in, gram_in, k_factor, c_factor, k_moment, c_moment, leads,
-    k_new, c_new, km_new, cm_new, k_half, c_half,
-):
-    f = lax.axis_index("fsdp")
-    flag = jnp.where(f > 0, 1.0, 0.0)
-    tokens = counts[0]
+        sums_all = sums_all + tr[i]
+    trace = [sums_all[i : i + 1, 0:1] for i in range(4)]
+    total_tokens = counts[0]
     for i in range(1, 8):
-        tokens = tokens + counts[i]
-    inverse = 1.0 / jnp.full((1, 1), tokens.astype(f32), f32)
+        total_tokens = total_tokens + counts[i]
+    inverse = 1.0 / jnp.full((1, 1), total_tokens.astype(f32), f32)
     width = 8192.0
-    trace = [traces[i : i + 1, 0:1] for i in range(4)]
-    rows = lax.broadcasted_iota(jnp.int32, (256, 256), 0)
-    cols = lax.broadcasted_iota(jnp.int32, (256, 256), 1)
     identity = jnp.where(rows == cols, 1.0, 0.0)
-    for side, (factor, moment, f_new, m_new, half) in enumerate(
-        ((k_factor, k_moment, k_new, km_new, k_half), (c_factor, c_moment, c_new, cm_new, c_half))
-    ):
+
+    def advance(side):
+        factor, moment = (k_factor, c_factor)[side], (k_moment, c_moment)[side]
+        f_new, m_new, half16 = (k_new, c_new)[side], (km_new, cm_new)[side], (k_half, c_half)[side]
         other_h = trace[2 - 2 * side] * inverse * inverse
         other_g = trace[3 - 2 * side] * damping
         diag = factor[0, :, 0:256]
         border = factor[0, :, 256:512] * flag
-        lead = leads[side * 256 : side * 256 + 256, :].astype(f32)
-        fresh = (other_h * h_in[side] + other_g * gram_in[side] - width * identity) / (2.0 * width)
-        cross = dot(lead.T, other_h * u_in[side] + other_g * border) * flag / (2.0 * width)
+        lead = lead_b[...].reshape(512, 256)[side * 256 : side * 256 + 256, :].astype(f32)
+        fresh = (other_h * h_out[side] + other_g * gram_out[side] - width * identity) / (2.0 * width)
+        cross = dot(lead.T, other_h * u_out[side] + other_g * border) * flag / (2.0 * width)
         m_diag = momentum_rate * moment[0, :, 0:256] + fresh
         m_side = (momentum_rate * moment[0, :, 256:512] + cross) * flag
         n_diag = diag - step_rate * dot(diag, m_diag)
@@ -492,36 +480,8 @@
         f_new[0, :, 256:512] = n_side
         m_new[0, :, 0:256] = m_diag
         m_new[0, :, 256:512] = m_side
-        half[0:256, :] = n_diag.astype(bf16)
-        half[256:512, :] = n_side.astype(bf16)
-
-
-def precond_body(
-    k_half, c_half, grad, grad_lead, out,
-    lead_src, lead_in, own, lead_sum, all_lead, second, lead_rows, cb, term, terms, part,
-    rs_s, rs_r, ga_s, ga_r, ca_s, ca_r, cz_s, cz_r, cx_s, cx_r, ro_s, ro_r, te_s, te_r,
-):
-    x, y, z, c = position()
-    d, f = lax.axis_index("dp"), lax.axis_index("fsdp")
-    barrier = pltpu.get_barrier_semaphore()
-
-    @pl.loop(1, 32)
-    def _(t):
-        greet(barrier, (d, lax.rem(f + t, 32)))
-
-    @pl.when(d == 0)
-    def _():
-        for t in range(1, 8):
-            greet(barrier, (t, f))
-
-    @pl.when(d > 0)
-    def _():
-        greet(barrier, (0, f))
-
-    k_diag, k_side = k_half[0:256, :], k_half[256:512, :]
-    first = (dot16(grad[...], k_diag) + dot16(grad_lead[...], k_side)).astype(bf16)
-    lead_src[...] = dot16(first, k_side.T).astype(bf16).reshape(32, 32, 256)
-    pl.semaphore_wait(barrier, 31 + jnp.where(d == 0, 7, 1))
+        half16[0:256, :] = n_diag.astype(bf16)
+        half16[256:512, :] = n_side.astype(bf16)
 
     holder = lax.div(z, 4) == c
     root = jnp.logical_and(holder, x == y)
@@ -534,19 +494,26 @@
         to = lax.rem(x + t, NX)
         return send(quarter(to), cb.at[to, j], ca_s.at[t], ca_r, (d, to * NZ + z))
 
+    advance(1)
+
     @pl.when(root)
     def _():
         for t in range(1, 4):
             scatter_copy(t).start()
         pltpu.make_async_copy(quarter(x), cb.at[x, j], ca_r).start()
 
-    own_piece = pltpu.make_async_copy(lead_src.at[f], lead_in.at[f], rs_r.at[0])
+    advance(0)
+    k_diag, k_side = k_half[0:256, :], k_half[256:512, :]
+    first = (dot16(grad[...], k_diag) + dot16(lead_g[...].reshape(1024, 256), k_side)).astype(bf16)
+    lead_src[...] = dot16(first, k_side.T).astype(bf16).reshape(32, 32, 256)
+
+    own_piece = pltpu.make_async_copy(lead_src.at[f], lead_in.at[f], bo_r.at[0])
     own_piece.start()
 
     @pl.loop(1, 32)
     def _(t):
         there = lax.rem(f + t, 32)
-        send(lead_src.at[there], lead_in.at[f], rs_s.at[t], rs_r.at[t], (d, there)).start()
+        send(lead_src.at[there], lead_in.at[f], bo_s.at[t], bo_r.at[t], (d, there)).start()
 
     own[...] = dot16(first, k_diag.T)
 
@@ -564,8 +531,8 @@
     @pl.loop(1, 32)
     def _(t):
         there = lax.rem(f + t, 32)
-        send(lead_src.at[there], lead_in.at[f], rs_s.at[t], rs_r.at[t], (d, there)).wait_send()
-        arrived(lead_in.at[lax.rem(f + 32 - t, 32)], rs_r.at[t])
+        send(lead_src.at[there], lead_in.at[f], bo_s.at[t], bo_r.at[t], (d, there)).wait_send()
+        arrived(lead_in.at[lax.rem(f + 32 - t, 32)], bo_r.at[t])
 
     total = lead_in[0].astype(f32)
     for i in range(1, 32):
@@ -656,40 +623,80 @@
     @pl.when(f > 0)
     def _():
         send(lead_sum, all_lead.at[f], ga_s, ga_r.at[f], (d, 0)).wait_send()
+    for on in passed:
+        on.wait_send()
+    for side in range(2):
+        y_copy(side).wait_send()
+        x_copy(side).wait_send()
+        for g in range(1, 4):
+            z_copy(side, g).wait_send()
+    for copies in tokens:
+        for i, at, one, two in copies:
+            if i > 0:
+                one.wait_send()
+                two.wait_send()
+
+    @pl.when(f == 0)
+    def _():
+        @pl.loop(1, 32)
+        def _(t):
+            send(grad_piece(t), piece_g, s3.at[t], r3.at[0], (d, t)).wait_send()
+            send(lead_piece(t), piece_b, s4.at[t], r3.at[1], (d, t)).wait_send()
+
+    for side in range(2):
+
+        @pl.when(mine == 0)
+        def _():
+            @pl.loop(0, 32)
+            def _(t):
+                @pl.when(jnp.logical_not(is_me(lead_target(t))))
+                def _():
+                    lead_send(side, t).wait_send()
+
+        for m in range(2):
+
+            @pl.when(jnp.logical_not(is_me((to_d, mine + 16 * m))))
+            def _():
+                rows_send(side, m).wait_send()
+
+        for i in range(2):
+            for t in range(4):
+                share_send(side, i, t).wait_send()
+            for t in range(1, 4):
+                pass_send(side, i, t).wait_send()
+
+
+def finish_body(*refs):
+    for src, dst in zip(refs[:5], refs[5:]):
+        dst[...] = src[...]
 
 
 def per_device(acts, out_grads, token_counts, k_factor, c_factor, k_moment, c_moment, grad_weight):
     SM = pl.BlockSpec(memory_space=pltpu.SMEM)
     V = pltpu.VMEM
-    h, u, grams, traces, leads, grad_lead = call(
-        stats_body, "stats",
-        (token_counts, acts, out_grads, k_factor, c_factor, grad_weight), [SM, ANY, ANY, VM, VM, ANY],
-        [((2, 256, 256), f32)] * 3 + [((8, 128), f32), ((512, 256), bf16), ((1024, 256), bf16)], [VM] * 6,
-        [V((2, 128, 8192), bf16), V((2, 16, 2, 64, 512), bf16), V((2, 2, 2, 64, 128), bf16),
+    results = [((1, 256, 512), f32)] * 4 + [((1024, 256), bf16)]
+    held = call(
+        step_body, "step",
+        (token_counts, acts, out_grads, k_factor, c_factor, k_moment, c_moment, grad_weight),
+        [SM, ANY, ANY] + [VM] * 5, results, [VM] * 5,
+        [V((2, 256, 256), f32), V((2, 256, 256), f32), V((2, 256, 256), f32),
+         V((32, 32, 256), bf16), V((32, 32, 256), bf16), V((1024, 256), f32), V((32, 256), bf16),
+         V((32, 32, 256), bf16), V((1024, 256), bf16), V((256, 256), bf16), V((4, 4, 128, 256), bf16),
+         V((256, 256), bf16), V((8, 256, 256), bf16), V((4, 256, 256), f32), V((512, 256), bf16), V((512, 256), bf16),
+         V((2, 128, 8192), bf16), V((2, 16, 2, 64, 512), bf16), V((2, 2, 2, 64, 128), bf16),
          V((2, 32, 64, 512), bf16), V((2, 32, 64, 256), bf16), V((512, 256), bf16), V((16, 256), bf16),
-         V((32, 256), bf16), V((2, 16, 4, 16, 256), bf16), V((2, 16, 4, 16, 256), bf16), V((2, 2, 2, 16, 256), bf16),
+         V((32, 256), bf16), V((2, 16, 4, 16, 256), bf16), V((2, 8, 4, 16, 256), bf16), V((2, 8, 4, 16, 256), bf16),
+         V((2, 4, 4, 16, 256), bf16), V((2, 4, 4, 16, 256), bf16), V((2, 4, 4, 16, 256), bf16), V((2, 2, 2, 16, 256), bf16),
          V((2, 16, 3, 16, 256), bf16), V((32, 8, 128), f32), V((4, 8, 16, 256), bf16), V((4, 8, 32, 256), bf16),
          DMA((2,))] + [DMA((2, 32))] * 6 + [DMA((32,)), DMA((32,)), DMA((2,)),
          DMA((2, 16)), DMA((2, 16)), DMA((2, 2)), DMA((2, 16)), DMA((2, 32)), DMA((2, 16)), DMA((2, 2, 4)),
          DMA((2, 2, 4)), DMA((8,)), DMA((8,)), DMA((8,)), DMA((8,)), DMA((4,)), DMA((4,)), DMA((4,)), DMA((4,)),
-         DMA((32,)), DMA((32,))],
-        1,
-    )
-    k_new, c_new, km_new, cm_new, k_half, c_half = call(
-        advance_body, "advance",
-        (token_counts, traces, h, u, grams, k_factor, c_factor, k_moment, c_moment, leads), [SM] + [VM] * 9,
-        [((1, 256, 512), f32)] * 4 + [((512, 256), bf16)] * 2, [VM] * 6,
-    )
-    (precond,) = call(
-        precond_body, "precond", (k_half, c_half, grad_weight, grad_lead), [VM] * 4, [((1024, 256), bf16)], [VM],
-        [V((32, 32, 256), bf16), V((32, 32, 256), bf16), V((1024, 256), f32), V((32, 256), bf16),
-         V((32, 32, 256), bf16), V((1024, 256), bf16), V((256, 256), bf16), V((4, 4, 128, 256), bf16),
-         V((256, 256), bf16), V((8, 256, 256), bf16), V((4, 256, 256), f32),
+         DMA((32,)), DMA((32,)),
          DMA((32,)), DMA((32,)), DMA, DMA((32,)), DMA((4,)), DMA, DMA((8,)), DMA((4,)), DMA((4,)), DMA((4,)),
          DMA((8,)), DMA, DMA, DMA((8,))],
-        2,
+        0,
     )
-    return k_new, c_new, km_new, cm_new, precond
+    return tuple(call(finish_body, "finish", held, [VM] * 5, results, [VM] * 5))
 
 
 def solution(mesh):

time: 170 us -> 151 us (0.89)
  Pallas kernels: 167 us -> 149 us
  local copies, waits for them, and re-layouts: 1.87 us -> 0 us
    pallas_call x3 -> x2, Pallas kernels: 167 us -> 149 us  [call(): pl.pallas_call(body, out_shape=[jax.ShapeDtypeStruct(s, t) for s, t in ou...]
    unnamed x1 -> x0, local copies, waits for them, and re-layouts: 1.87 us -> none
where the time goes in v4:
time: 151 us; the launch traced here: 150 us
  Pallas kernels  149 us (99%)
    pallas_call x2, Pallas kernels, call(): pl.pallas_call(body, out_shape=[jax.ShapeDtypeStruct(s, t) for s, t in ou...  149 us

profile of v4, /device:TPU:0, one launch (start us, length us, event | category | flops | bytes accessed | tf_op | source)
XLA Modules:
  0.0 150.0 jit_solution(2963454516055111491)
XLA Ops:
  0.6 146.2 %step.1 = (f32[1,256,512]{2,1,0:T(8,128)}, f32[1,256,512]{2,1,0:T(8,128)}, f32[1,256,512]{2,1,0:T(8,128)}, f32[1,256,512]{2,1,0:T(8,128)}, bf16[1024,256]{1,0:T(8,128)(2,1)}) custom-call(s32[8]{0:T(128)} %counts.1, bf16[128,8192]{1,0:T(8,128)(2,1)} %acts.1, bf16[128,8192]{1,0:T(8,128)(2,1)} %grads.1, f32[1,256,512]{2,1,0:T(8,128)} %k_factor.1, ...), custom_call_target="tpu_custom_call" | custom-call | tf_op jit(solution)/shard_map/step/pallas_call | solution.py:57
  146.8 3.2 %finish.1 = (f32[1,256,512]{2,1,0:T(8,128)}, f32[1,256,512]{2,1,0:T(8,128)}, f32[1,256,512]{2,1,0:T(8,128)}, f32[1,256,512]{2,1,0:T(8,128)}, bf16[1024,256]{1,0:T(8,128)(2,1)}) custom-call(f32[1,256,512]{2,1,0:T(8,128)} %get-tuple-element.10.refs_0_, f32[1,256,512]{2,1,0:T(8,128)} %get-tuple-element.11.refs_1_, f32[1,256,512]{2,1,0:T(8,128)} %get-tuple-element.12.refs_2_, ...), custom_call_target="tpu_custom_call" | custom-call | tf_op jit(solution)/shard_map/finish/pallas_call | solution.py:57

commit v5 on v4

--- a/solution.py
+++ b/solution.py
@@ -83,11 +83,11 @@
 
 def step_body(
     counts, acts, grads, k_factor, c_factor, k_moment, c_moment, grad, k_new, c_new, km_new, cm_new, out,
-    h_out, u_out, gram_out, lead_src, lead_in, own, lead_sum, all_lead, second, lead_rows, cb, term, terms, part, k_half,
+    h_out, u_out, v_out, gram_out, lead_src, lead_in, lead_x, lead_z, own, lead_sum, all_lead, second, lead_rows, cb, term, terms, part, k_half,
     c_half, raw, xs, ls, xc, x0, b0, piece_b, piece_g, ps, py_in, qx, px_in, qz, pz_in, sm, st, tr, lead_b, lead_g,
     in_s, s1, r1, s2, r2, s5, r4, s3, s4, r3,
     rs_s, rs_r, de_s, de_r, a0_s, a0_r, ag_s, fw_s, zb_s, zb_r, zg_s, zg_r, xb_s, xb_r, xg_s, xg_r, tr_s, tr_r,
-    bo_s, bo_r, ga_s, ga_r, ca_s, ca_r, cz_s, cz_r, cx_s, cx_r, ro_s, ro_r, te_s, te_r,
+    bo_s, bo_r, bz_s, bz_r, ga_s, ga_r, ca_s, ca_r, cz_s, cz_r, cx_s, cx_r, ro_s, ro_r, te_s, te_r,
 ):
     x, y, z, c = position()
     d, f = lax.axis_index("dp"), lax.axis_index("fsdp")
@@ -108,7 +108,7 @@
     offsets = [(a, b, g, e) for a in (0, 1) for b in (0, 1) for g in (0, 1) for e in (0, 1)]
     mine = class_of(x, y, z, c)
     xi, yi, zi = lax.div(x, 2), lax.div(y, 2), lax.div(z, 2)
-    slot = yi * 8 + xi * 4 + zi
+    slot = (yi * 8 + xi * 4 + zi, xi * 8 + yi * 4 + zi)
     mate_y = device(x, lax.rem(y + 2, NY), z, c)
     mate_x = device(lax.rem(x + 2, NX), y, z, c)
 
@@ -121,16 +121,17 @@
     def group_for(parity):
         return lax.rem(2 * yi + parity + lax.rem(zi, 2), NY) * 2 + lax.div(zi, 2)
 
-    def slots_at(there_y):
+    def slots_at(there_y, side):
         shift = lax.rem(there_y + py, 2)
-        low = lax.div(lax.rem(there_y - shift + NY, NY), 2) * 8 + 2 * c + shift
-        return [low, low + 4]
+        half_y = lax.div(lax.rem(there_y - shift + NY, NY), 2)
+        low = half_y * (8, 4)[side] + 2 * c + shift
+        return [low, low + (4, 8)[side]]
 
     def owner(j, qx, qy, qz, qc):
         return device(qx + 2 * lax.rem(lax.div(j, 4), 2), qy + 2 * lax.div(j, 8), qz + 2 * lax.rem(j, 4), qc)
 
     to_d = group_for(lax.rem(y, 2))
-    from_j = slots_at(y)
+    from_j = [slots_at(y, side) for side in range(2)]
 
     def is_me(there):
         return jnp.logical_and(there[0] == d, there[1] == f)
@@ -152,7 +153,7 @@
 
     for t in range(1, 4):
         greet(barrier, device(x, lax.rem(y + t, NY), z, c))
-    for j in from_j:
+    for j in from_j[0]:
         for there in (owner(j, px, py, pz, pc), owner(j, 0, 0, 0, 0)):
 
             @pl.when(jnp.logical_not(is_me(there)))
@@ -278,35 +279,38 @@
             g = lax.dot_general(left, right, dims, preferred_element_type=f32)
             ps[side, :, i, :, :] = g.astype(bf16).reshape(16, 16, 256)
 
-    def y_copy(side):
-        src = ps.at[side, pl.ds((1 - yi) * 8, 8)]
-        return send(src, py_in.at[side], rs_s.at[side, 0], rs_r.at[side, 0], mate_y)
-
-    def x_copy(side):
-        src = qx.at[side, pl.ds((1 - xi) * 4, 4)]
-        return send(src, px_in.at[side], rs_s.at[side, 1], rs_r.at[side, 1], mate_x)
+    bits = ((yi, xi), (xi, yi))
+    halves = ((mate_y, mate_x), (mate_x, mate_y))
+
+    def half_copy(side):
+        src = ps.at[side, pl.ds((1 - bits[side][0]) * 8, 8)]
+        return send(src, py_in.at[side], rs_s.at[side, 0], rs_r.at[side, 0], halves[side][0])
+
+    def quarter_copy(side):
+        src = qx.at[side, pl.ds((1 - bits[side][1]) * 4, 4)]
+        return send(src, px_in.at[side], rs_s.at[side, 1], rs_r.at[side, 1], halves[side][1])
 
     def z_copy(side, g):
         src = qz.at[side, lax.rem(zi + g, 4)]
         return send(src, pz_in.at[side, g], rs_s.at[side, 1 + g], rs_r.at[side, 1 + g], mate_z(g))
 
-    def over_x(side):
+    def over_half(side):
         arrived(py_in.at[side], rs_r.at[side, 0])
-        qx[side] = (ps[side, pl.ds(yi * 8, 8)].astype(f32) + py_in[side].astype(f32)).astype(bf16)
-        x_copy(side).start()
-
-    def over_z(side):
+        qx[side] = (ps[side, pl.ds(bits[side][0] * 8, 8)].astype(f32) + py_in[side].astype(f32)).astype(bf16)
+        quarter_copy(side).start()
+
+    def over_quarter(side):
         arrived(px_in.at[side], rs_r.at[side, 1])
-        qz[side] = (qx[side, pl.ds(xi * 4, 4)].astype(f32) + px_in[side].astype(f32)).astype(bf16)
+        qz[side] = (qx[side, pl.ds(bits[side][1] * 4, 4)].astype(f32) + px_in[side].astype(f32)).astype(bf16)
         for g in range(1, 4):
             z_copy(side, g).start()
 
     passed = collect(0, tokens[0])
     gram(0)
-    y_copy(0).start()
+    half_copy(0).start()
     passed += collect(1, tokens[1])
     gram(1)
-    y_copy(1).start()
+    half_copy(1).start()
     def total(side):
         value = qz[side, zi].astype(f32)
         for g in range(1, 4):
@@ -318,11 +322,11 @@
                 sm[side, m, q] = value[2 * q + m]
 
     def lead_send(side, t):
-        return send(sm.at[side, 0, 0], st.at[side, slot, 2], a0_s.at[side, t], a0_r.at[side, slot], lead_target(t))
+        return send(sm.at[side, 0, 0], st.at[side, slot[side], 2], a0_s.at[side, t], a0_r.at[side, slot[side]], lead_target(t))
 
     def rows_send(side, m):
         there = (to_d, mine + 16 * m)
-        return send(sm.at[side, m], st.at[side, slot, 0:2], de_s.at[side, m], de_r.at[side, slot], there)
+        return send(sm.at[side, m], st.at[side, slot[side], 0:2], de_s.at[side, m], de_r.at[side, slot[side]], there)
 
     def deliver(side):
         @pl.when(mine == 0)
@@ -333,7 +337,7 @@
 
                 @pl.when(me)
                 def _():
-                    pltpu.make_async_copy(sm.at[side, 0, 0], st.at[side, slot, 2], a0_r.at[side, slot]).start()
+                    pltpu.make_async_copy(sm.at[side, 0, 0], st.at[side, slot[side], 2], a0_r.at[side, slot[side]]).start()
 
                 @pl.when(jnp.logical_not(me))
                 def _():
@@ -344,7 +348,7 @@
 
             @pl.when(me)
             def _():
-                pltpu.make_async_copy(sm.at[side, m], st.at[side, slot, 0:2], de_r.at[side, slot]).start()
+                pltpu.make_async_copy(sm.at[side, m], st.at[side, slot[side], 0:2], de_r.at[side, slot[side]]).start()
 
             @pl.when(jnp.logical_not(me))
             def _():
@@ -352,28 +356,28 @@
 
     def share_send(side, i, t):
         there = device(x, lax.rem(y + t, NY), z, c) if t > 0 else partner
-        at = st.at[side, from_j[i]]
-        return send(at, at, ag_s.at[side, i, t], de_r.at[side, from_j[i]], there)
+        at = st.at[side, from_j[side][i]]
+        return send(at, at, ag_s.at[side, i, t], de_r.at[side, from_j[side][i]], there)
 
     def pass_send(side, i, t):
-        j = slots_at(lax.rem(y + NY - t, NY))[i]
+        j = slots_at(lax.rem(y + NY - t, NY), side)[i]
         return send(st.at[side, j], st.at[side, j], fw_s.at[side, i, t], de_r.at[side, j], partner)
 
     def share(side):
         for i in range(2):
-            arrived(st.at[side, from_j[i], 0:2], de_r.at[side, from_j[i]])
-            arrived(st.at[side, from_j[i], 2], a0_r.at[side, from_j[i]])
+            arrived(st.at[side, from_j[side][i], 0:2], de_r.at[side, from_j[side][i]])
+            arrived(st.at[side, from_j[side][i], 2], a0_r.at[side, from_j[side][i]])
             for t in (1, 2, 3, 0):
                 share_send(side, i, t).start()
 
     def pass_on(side):
         for t in (1, 3, 2):
             for i in range(2):
-                j = slots_at(lax.rem(y + NY - t, NY))[i]
+                j = slots_at(lax.rem(y + NY - t, NY), side)[i]
                 arrived(st.at[side, j], de_r.at[side, j])
                 pass_send(side, i, t).start()
 
-    over_x(0)
+    over_half(0)
     arrived(piece_g, r3.at[0])
     arrived(piece_b, r3.at[1])
     own_b = pltpu.make_async_copy(piece_b, lead_b.at[x, z], zb_r.at[0])
@@ -384,9 +388,9 @@
         there = (d, x * NZ + lax.rem(z + t, NZ))
         send(piece_b, lead_b.at[x, z], zb_s.at[t], zb_r.at[t], there).start()
         send(piece_g, lead_g.at[x, z], zg_s.at[t], zg_r.at[t], there).start()
-    over_x(1)
-    over_z(0)
-    over_z(1)
+    over_half(1)
+    over_quarter(0)
+    over_quarter(1)
     total(0)
     deliver(0)
     total(1)
@@ -426,10 +430,10 @@
         lead = st[side, :, 2].reshape(256, 256)
         u = dot16(cross, diag16) + dot16(lead, border16)
         v = dot16(a, diag16) + dot16(cross.T, border16)
-        h = dot(diag16.astype(f32).T, v) + dot(border16.astype(f32).T, u)
+        tr_h = jnp.sum(diag16.astype(f32) * v) + jnp.sum(border16.astype(f32) * u)
+        tr[f, side * 2 : side * 2 + 1, :] = jnp.full((1, 128), tr_h, f32)
         u_out[side] = u
-        h_out[side] = h
-        tr[f, side * 2 : side * 2 + 1, :] = jnp.full((1, 128), jnp.sum(jnp.where(rows == cols, h, 0.0)), f32)
+        v_out[side] = v
 
     second_moment(0)
     second_moment(1)
@@ -437,6 +441,11 @@
     @pl.loop(1, 32)
     def _(t):
         send(tr.at[f], tr.at[f], tr_s.at[t], tr_r.at[t], (d, lax.rem(f + t, 32))).start()
+
+    for side, factor in enumerate((k_factor, c_factor)):
+        diag16 = factor[0, :, 0:256].astype(bf16)
+        border16 = (factor[0, :, 256:512] * flag).astype(bf16)
+        h_out[side] = dot(diag16.astype(f32).T, v_out[side]) + dot(border16.astype(f32).T, u_out[side])
 
     for t in range(1, 4):
         there = (d, lax.rem(x + t, NX) * NZ + z)
@@ -507,13 +516,17 @@
     first = (dot16(grad[...], k_diag) + dot16(lead_g[...].reshape(1024, 256), k_side)).astype(bf16)
     lead_src[...] = dot16(first, k_side.T).astype(bf16).reshape(32, 32, 256)
 
-    own_piece = pltpu.make_async_copy(lead_src.at[f], lead_in.at[f], bo_r.at[0])
-    own_piece.start()
-
-    @pl.loop(1, 32)
-    def _(t):
-        there = lax.rem(f + t, 32)
-        send(lead_src.at[there], lead_in.at[f], bo_s.at[t], bo_r.at[t], (d, there)).start()
+    def border_x(t):
+        to = lax.rem(x + t, NX)
+        src = lead_src.at[pl.ds(pl.multiple_of(to * 8, 8), 8)]
+        return send(src, lead_in.at[t], bo_s.at[t], bo_r.at[t], (d, to * NZ + z))
+
+    def border_z(t):
+        to = lax.rem(z + t, NZ)
+        return send(lead_x.at[to], lead_z.at[t], bz_s.at[t], bz_r.at[t], (d, x * NZ + to))
+
+    for t in (1, 3, 2):
+        border_x(t).start()
 
     own[...] = dot16(first, k_diag.T)
 
@@ -526,23 +539,14 @@
         for t in range(1, 8):
             ring_copy(t).start()
 
-    own_piece.wait()
-
-    @pl.loop(1, 32)
-    def _(t):
-        there = lax.rem(f + t, 32)
-        send(lead_src.at[there], lead_in.at[f], bo_s.at[t], bo_r.at[t], (d, there)).wait_send()
-        arrived(lead_in.at[lax.rem(f + 32 - t, 32)], bo_r.at[t])
-
-    total = lead_in[0].astype(f32)
-    for i in range(1, 32):
-        total = total + lead_in[i].astype(f32)
-    lead_sum[...] = total.astype(bf16)
+    border = lead_src[pl.ds(pl.multiple_of(x * 8, 8), 8)].astype(f32)
+    for t in (1, 3, 2):
+        arrived(lead_in.at[t], bo_r.at[t])
+        border = border + lead_in[t].astype(f32)
+    lead_x[...] = border.astype(bf16)
+    for t in range(1, 8):
+        border_z(t).start()
     second[...] = own[...].astype(bf16)
-
-    @pl.when(f > 0)
-    def _():
-        send(lead_sum, all_lead.at[f], ga_s, ga_r.at[f], (d, 0)).start()
 
     for i in range(4):
 
@@ -550,11 +554,25 @@
         def _():
             arrived(cb.at[x, i], cz_r.at[i])
 
-    def spread_copy(t):
-        return send(cb.at[x], cb.at[x], cx_s.at[t], cx_r.at[t], (d, lax.rem(x + t, NX) * NZ + z))
-
-    for t in range(1, 4):
-        spread_copy(t).start()
+    def spread_copy(t, low):
+        at = cb.at[x, 2 * low : 2 * low + 2]
+        return send(at, at, cx_s.at[low, t], cx_r.at[low, t], (d, lax.rem(x + t, NX) * NZ + z))
+
+    for t in (1, 3):
+        spread_copy(t, 0).start()
+
+    total = lead_x[z].astype(f32)
+    for t in range(1, 8):
+        arrived(lead_z.at[t], bz_r.at[t])
+        total = total + lead_z[t].astype(f32)
+    lead_sum[...] = total.astype(bf16)
+
+    @pl.when(f > 0)
+    def _():
+        send(lead_sum, all_lead.at[f], ga_s, ga_r.at[f], (d, 0)).start()
+
+    for t, low in ((1, 1), (3, 1), (2, 0), (2, 1)):
+        spread_copy(t, low).start()
 
     @pl.when(f == 0)
     def _():
@@ -572,7 +590,8 @@
         pltpu.make_async_copy(src, lead_rows, ro_r).start()
 
     for t in range(1, 4):
-        arrived(cb.at[lax.rem(x + NX - t, NX)], cx_r.at[t])
+        for low in range(2):
+            arrived(cb.at[lax.rem(x + NX - t, NX), 2 * low : 2 * low + 2], cx_r.at[low, t])
     for i in range(4):
         diag = cb[0:2, i].reshape(256, 256)
         part[i] = dot16(diag.T, second[i * 256 : i * 256 + 256, :])
@@ -618,7 +637,11 @@
             ring_copy(t).wait_send()
 
     for t in range(1, 4):
-        spread_copy(t).wait_send()
+        spread_copy(t, 0).wait_send()
+        spread_copy(t, 1).wait_send()
+        border_x(t).wait_send()
+    for t in range(1, 8):
+        border_z(t).wait_send()
 
     @pl.when(f > 0)
     def _():
@@ -626,8 +649,8 @@
     for on in passed:
         on.wait_send()
     for side in range(2):
-        y_copy(side).wait_send()
-        x_copy(side).wait_send()
+        half_copy(side).wait_send()
+        quarter_copy(side).wait_send()
         for g in range(1, 4):
             z_copy(side, g).wait_send()
     for copies in tokens:
@@ -679,8 +702,9 @@
         step_body, "step",
         (token_counts, acts, out_grads, k_factor, c_factor, k_moment, c_moment, grad_weight),
         [SM, ANY, ANY] + [VM] * 5, results, [VM] * 5,
-        [V((2, 256, 256), f32), V((2, 256, 256), f32), V((2, 256, 256), f32),
-         V((32, 32, 256), bf16), V((32, 32, 256), bf16), V((1024, 256), f32), V((32, 256), bf16),
+        [V((2, 256, 256), f32), V((2, 256, 256), f32), V((2, 256, 256), f32), V((2, 256, 256), f32),
+         V((32, 32, 256), bf16), V((4, 8, 32, 256), bf16), V((8, 32, 256), bf16), V((8, 32, 256), bf16),
+         V((1024, 256), f32), V((32, 256), bf16),
          V((32, 32, 256), bf16), V((1024, 256), bf16), V((256, 256), bf16), V((4, 4, 128, 256), bf16),
          V((256, 256), bf16), V((8, 256, 256), bf16), V((4, 256, 256), f32), V((512, 256), bf16), V((512, 256), bf16),
          V((2, 128, 8192), bf16), V((2, 16, 2, 64, 512), bf16), V((2, 2, 2, 64, 128), bf16),
@@ -692,7 +716,7 @@
          DMA((2, 16)), DMA((2, 16)), DMA((2, 2)), DMA((2, 16)), DMA((2, 32)), DMA((2, 16)), DMA((2, 2, 4)),
          DMA((2, 2, 4)), DMA((8,)), DMA((8,)), DMA((8,)), DMA((8,)), DMA((4,)), DMA((4,)), DMA((4,)), DMA((4,)),
          DMA((32,)), DMA((32,)),
-         DMA((32,)), DMA((32,)), DMA, DMA((32,)), DMA((4,)), DMA, DMA((8,)), DMA((4,)), DMA((4,)), DMA((4,)),
+         DMA((4,)), DMA((4,)), DMA((8,)), DMA((8,)), DMA, DMA((32,)), DMA((4,)), DMA, DMA((8,)), DMA((4,)), DMA((2, 4)), DMA((2, 4)),
          DMA((8,)), DMA, DMA, DMA((8,))],
         0,
     )

time: 151 us -> 143 us (0.947)
  Pallas kernels: 149 us -> 142 us
    pallas_call x2, Pallas kernels: 149 us -> 142 us  [call(): pl.pallas_call(body, out_shape=[jax.ShapeDtypeStruct(s, t) for s, t in ou...]
where the time goes in v5:
time: 143 us
  Pallas kernels  142 us (99%)
    pallas_call x2, Pallas kernels, call(): pl.pallas_call(body, out_shape=[jax.ShapeDtypeStruct(s, t) for s, t in ou...  142 us

profile of v5, /device:TPU:0, one launch (start us, length us, event | category | flops | bytes accessed | tf_op | source)
XLA Modules:
  0.0 142.7 jit_solution(3445668791130224063)
XLA Ops:
  0.6 138.8 %step.1 = (f32[1,256,512]{2,1,0:T(8,128)}, f32[1,256,512]{2,1,0:T(8,128)}, f32[1,256,512]{2,1,0:T(8,128)}, f32[1,256,512]{2,1,0:T(8,128)}, bf16[1024,256]{1,0:T(8,128)(2,1)}) custom-call(s32[8]{0:T(128)} %counts.1, bf16[128,8192]{1,0:T(8,128)(2,1)} %acts.1, bf16[128,8192]{1,0:T(8,128)(2,1)} %grads.1, f32[1,256,512]{2,1,0:T(8,128)} %k_factor.1, ...), custom_call_target="tpu_custom_call" | custom-call | tf_op jit(solution)/shard_map/step/pallas_call | solution.py:57
  139.5 3.2 %finish.1 = (f32[1,256,512]{2,1,0:T(8,128)}, f32[1,256,512]{2,1,0:T(8,128)}, f32[1,256,512]{2,1,0:T(8,128)}, f32[1,256,512]{2,1,0:T(8,128)}, bf16[1024,256]{1,0:T(8,128)(2,1)}) custom-call(f32[1,256,512]{2,1,0:T(8,128)} %get-tuple-element.10.refs_0_, f32[1,256,512]{2,1,0:T(8,128)} %get-tuple-element.11.refs_1_, f32[1,256,512]{2,1,0:T(8,128)} %get-tuple-element.12.refs_2_, ...), custom_call_target="tpu_custom_call" | custom-call | tf_op jit(solution)/shard_map/finish/pallas_call | solution.py:57

commit v6 on v5

--- a/solution.py
+++ b/solution.py
@@ -83,7 +83,7 @@
 
 def step_body(
     counts, acts, grads, k_factor, c_factor, k_moment, c_moment, grad, k_new, c_new, km_new, cm_new, out,
-    h_out, u_out, v_out, gram_out, lead_src, lead_in, lead_x, lead_z, own, lead_sum, all_lead, second, lead_rows, cb, term, terms, part, k_half,
+    held, held_s, h_out, u_out, v_out, gram_out, lead_src, lead_in, lead_x, lead_z, own, lead_sum, all_lead, second, lead_rows, cb, term, terms, part, k_half,
     c_half, raw, xs, ls, xc, x0, b0, piece_b, piece_g, ps, py_in, qx, px_in, qz, pz_in, sm, st, tr, lead_b, lead_g,
     in_s, s1, r1, s2, r2, s5, r4, s3, s4, r3,
     rs_s, rs_r, de_s, de_r, a0_s, a0_r, ag_s, fw_s, zb_s, zb_r, zg_s, zg_r, xb_s, xb_r, xg_s, xg_r, tr_s, tr_r,
@@ -473,7 +473,7 @@
 
     def advance(side):
         factor, moment = (k_factor, c_factor)[side], (k_moment, c_moment)[side]
-        f_new, m_new, half16 = (k_new, c_new)[side], (km_new, cm_new)[side], (k_half, c_half)[side]
+        half16 = (k_half, c_half)[side]
         other_h = trace[2 - 2 * side] * inverse * inverse
         other_g = trace[3 - 2 * side] * damping
         diag = factor[0, :, 0:256]
@@ -485,10 +485,10 @@
         m_side = (momentum_rate * moment[0, :, 256:512] + cross) * flag
         n_diag = diag - step_rate * dot(diag, m_diag)
         n_side = (border - step_rate * (dot(lead, m_side) + dot(border, m_diag))) * flag
-        f_new[0, :, 0:256] = n_diag
-        f_new[0, :, 256:512] = n_side
-        m_new[0, :, 0:256] = m_diag
-        m_new[0, :, 256:512] = m_side
+        held[side, :, 0:256] = n_diag
+        held[side, :, 256:512] = n_side
+        held[2 + side, :, 0:256] = m_diag
+        held[2 + side, :, 256:512] = m_side
         half16[0:256, :] = n_diag.astype(bf16)
         half16[256:512, :] = n_side.astype(bf16)
 
@@ -512,6 +512,9 @@
         pltpu.make_async_copy(quarter(x), cb.at[x, j], ca_r).start()
 
     advance(0)
+    stores = [
+        pltpu.make_async_copy(held.at[i], ref.at[0], held_s.at[i]) for i, ref in enumerate((k_new, c_new, km_new, cm_new))
+    ]
     k_diag, k_side = k_half[0:256, :], k_half[256:512, :]
     first = (dot16(grad[...], k_diag) + dot16(lead_g[...].reshape(1024, 256), k_side)).astype(bf16)
     lead_src[...] = dot16(first, k_side.T).astype(bf16).reshape(32, 32, 256)
@@ -527,6 +530,8 @@
 
     for t in (1, 3, 2):
         border_x(t).start()
+    for store in stores:
+        store.start()
 
     own[...] = dot16(first, k_diag.T)
 
@@ -571,8 +576,19 @@
     def _():
         send(lead_sum, all_lead.at[f], ga_s, ga_r.at[f], (d, 0)).start()
 
-    for t, low in ((1, 1), (3, 1), (2, 0), (2, 1)):
-        spread_copy(t, low).start()
+    def came(t, low):
+        return cb.at[lax.rem(x + NX - t, NX), 2 * low : 2 * low + 2]
+
+    def relay_copy(t):
+        low = t // 2
+        at = came(t, low)
+        return send(at, at, cx_s.at[low, 2], cx_r.at[low, 2], (d, lax.rem(x + t, NX) * NZ + z))
+
+    for t in (1, 3):
+        spread_copy(t, 1).start()
+    for t in (1, 3):
+        arrived(came(t, t // 2), cx_r.at[t // 2, t])
+        relay_copy(t).start()
 
     @pl.when(f == 0)
     def _():
@@ -589,9 +605,8 @@
             send(src, lead_rows, ro_s.at[t], ro_r, (t, f)).start()
         pltpu.make_async_copy(src, lead_rows, ro_r).start()
 
-    for t in range(1, 4):
-        for low in range(2):
-            arrived(cb.at[lax.rem(x + NX - t, NX), 2 * low : 2 * low + 2], cx_r.at[low, t])
+    for t, low in ((1, 1), (3, 0), (2, 0), (2, 1)):
+        arrived(came(t, low), cx_r.at[low, t])
     for i in range(4):
         diag = cb[0:2, i].reshape(256, 256)
         part[i] = dot16(diag.T, second[i * 256 : i * 256 + 256, :])
@@ -636,9 +651,11 @@
         for t in range(1, 8):
             ring_copy(t).wait_send()
 
-    for t in range(1, 4):
+    for t in (1, 3):
         spread_copy(t, 0).wait_send()
         spread_copy(t, 1).wait_send()
+        relay_copy(t).wait_send()
+    for t in range(1, 4):
         border_x(t).wait_send()
     for t in range(1, 8):
         border_z(t).wait_send()
@@ -646,6 +663,8 @@
     @pl.when(f > 0)
     def _():
         send(lead_sum, all_lead.at[f], ga_s, ga_r.at[f], (d, 0)).wait_send()
+    for store in stores:
+        store.wait()
     for on in passed:
         on.wait_send()
     for side in range(2):
@@ -690,8 +709,21 @@
 
 
 def finish_body(*refs):
-    for src, dst in zip(refs[:5], refs[5:]):
-        dst[...] = src[...]
+    buffers, flat, sems = refs[10:]
+    moves = []
+    for i in range(5):
+        src, dst = (refs[i].at[0], refs[5 + i].at[0]) if i < 4 else (refs[i], refs[5 + i])
+        middle = buffers.at[i] if i < 4 else flat
+        moves.append(
+            (pltpu.make_async_copy(src, middle, sems.at[0, i]), pltpu.make_async_copy(middle, dst, sems.at[1, i]))
+        )
+    for load, _ in moves:
+        load.start()
+    for load, store in moves:
+        load.wait()
+        store.start()
+    for _, store in moves:
+        store.wait()
 
 
 def per_device(acts, out_grads, token_counts, k_factor, c_factor, k_moment, c_moment, grad_weight):
@@ -701,8 +733,8 @@
     held = call(
         step_body, "step",
         (token_counts, acts, out_grads, k_factor, c_factor, k_moment, c_moment, grad_weight),
-        [SM, ANY, ANY] + [VM] * 5, results, [VM] * 5,
-        [V((2, 256, 256), f32), V((2, 256, 256), f32), V((2, 256, 256), f32), V((2, 256, 256), f32),
+        [SM, ANY, ANY] + [VM] * 5, results, [ANY] * 4 + [VM],
+        [V((4, 256, 512), f32), DMA((4,)), V((2, 256, 256), f32), V((2, 256, 256), f32), V((2, 256, 256), f32), V((2, 256, 256), f32),
          V((32, 32, 256), bf16), V((4, 8, 32, 256), bf16), V((8, 32, 256), bf16), V((8, 32, 256), bf16),
          V((1024, 256), f32), V((32, 256), bf16),
          V((32, 32, 256), bf16), V((1024, 256), bf16), V((256, 256), bf16), V((4, 4, 128, 256), bf16),
@@ -720,7 +752,8 @@
          DMA((8,)), DMA, DMA, DMA((8,))],
         0,
     )
-    return tuple(call(finish_body, "finish", held, [VM] * 5, results, [VM] * 5))
+    scratch = [V((4, 256, 512), f32), V((1024, 256), bf16), DMA((2, 5))]
+    return tuple(call(finish_body, "finish", held, [ANY] * 5, results, [ANY] * 5, scratch))
 
 
 def solution(mesh):

time: 143 us -> 140 us (0.979)
  Pallas kernels: 142 us -> 139 us
    pallas_call x2, Pallas kernels: 142 us -> 139 us  [call(): pl.pallas_call(body, out_shape=[jax.ShapeDtypeStruct(s, t) for s, t in ou...]
where the time goes in v6:
time: 140 us
  Pallas kernels  139 us (99%)
    pallas_call x2, Pallas kernels, call(): pl.pallas_call(body, out_shape=[jax.ShapeDtypeStruct(s, t) for s, t in ou...  139 us

profile of v6, /device:TPU:0, one launch (start us, length us, event | category | flops | bytes accessed | tf_op | source)
XLA Modules:
  0.0 140.1 jit_solution(15010150989652167078)
XLA Ops:
  0.6 136.7 %step.1 = (f32[1,256,512]{2,1,0:T(8,128)}, f32[1,256,512]{2,1,0:T(8,128)}, f32[1,256,512]{2,1,0:T(8,128)}, f32[1,256,512]{2,1,0:T(8,128)}, bf16[1024,256]{1,0:T(8,128)(2,1)}) custom-call(s32[8]{0:T(128)} %counts.1, bf16[128,8192]{1,0:T(8,128)(2,1)} %acts.1, bf16[128,8192]{1,0:T(8,128)(2,1)} %grads.1, f32[1,256,512]{2,1,0:T(8,128)} %k_factor.1, ...), custom_call_target="tpu_custom_call" | custom-call | tf_op jit(solution)/shard_map/step/pallas_call | solution.py:57
  137.4 2.6 %finish.1 = (f32[1,256,512]{2,1,0:T(8,128)}, f32[1,256,512]{2,1,0:T(8,128)}, f32[1,256,512]{2,1,0:T(8,128)}, f32[1,256,512]{2,1,0:T(8,128)}, bf16[1024,256]{1,0:T(8,128)(2,1)}) custom-call(f32[1,256,512]{2,1,0:T(8,128)} %get-tuple-element.10.refs_0_, f32[1,256,512]{2,1,0:T(8,128)} %get-tuple-element.11.refs_1_, f32[1,256,512]{2,1,0:T(8,128)} %get-tuple-element.12.refs_2_, ...), custom_call_target="tpu_custom_call" | custom-call | tf_op jit(solution)/shard_map/finish/pallas_call | solution.py:57
